TPU v7x, 256 devices: a whole 4x4x8 slice. The times are simulated.
256 devices in a mesh: section: 4 (over x_lo, core), ctx: 64 (over y, x_hi, z).
Axes of the slice: x: 4 (x_hi: 2, x_lo: 2; x = x_hi * 2 + x_lo), y: 4, z: 8, core: 2. Of those that a mesh axis runs over, the one named last changes fastest.
Arguments:
- block_order: int32 [64], replicated, may hold values from 0 to 63, each once
- queries: bfloat16 [4, 512, 2560], P('section', 'ctx'), may hold values from -400 to 400
- cache_keys: bfloat16 [8192, 2560], P('ctx', 'section'), may hold values from -6 to 6
- cache_values: bfloat16 [8192, 2560], P('ctx', 'section'), may hold values from -6 to 6
- attention_out: bfloat16 [4, 512, 2560], P('section', 'ctx'), may hold values from -6 to 6
- output_grad: bfloat16 [4, 512, 2560], P('section', 'ctx'), may hold values from -1536 to 1536
Outputs:
- grad_queries: bfloat16 [4, 512, 2560], P('section', 'ctx')
- grad_keys: bfloat16 [8192, 2560], P('ctx', 'section')
- grad_values: bfloat16 [8192, 2560], P('ctx', 'section')
Inputs may be any that keep to these rules, and one draw needn't show every extreme that they name: `block_order`: every block number once.
All inputs are finite; a program needn't handle non-finite values.
Results may differ from a plain program's by a relative error of at most 0.012.
Values may be sent and summed in bfloat16 or wider, within the bound.
A program may use at most 64 MiB of HBM per device.

v0:
```python
import jax
import jax.numpy as jnp
from jax import lax
from jax.sharding import PartitionSpec as P

HEADS = 20
HEAD_DIM = 128


masked_score = -1e30


def local(block_order, queries, cache_keys, cache_values, attention_out, output_grad):
    ctx_count = lax.axis_size("ctx")
    rows_here = queries.shape[1]
    key_count = cache_keys.shape[0]
    key_total = key_count * ctx_count
    query_count = rows_here * ctx_count
    scaling = HEAD_DIM ** (-0.5)
    product = output_grad.astype(jnp.float32) * attention_out.astype(jnp.float32)
    delta_terms = jnp.sum(product.reshape(1, rows_here, HEADS, HEAD_DIM), axis=3)
    query_part, grad_part, delta_part = (queries, output_grad, delta_terms)
    key_block, value_block = (
        lax.all_gather(cache_keys, "section", axis=1, tiled=True),
        lax.all_gather(cache_values, "section", axis=1, tiled=True),
    )
    group_heads = HEADS
    layers = query_part.shape[0]
    pair_count = layers * group_heads
    query_all, grad_all = (
        lax.all_gather(query_part, "ctx", axis=1, tiled=True),
        lax.all_gather(grad_part, "ctx", axis=1, tiled=True),
    )
    delta_all = lax.all_gather(delta_part, "ctx", axis=1, tiled=True)

    def split_heads(values):
        return (
            values.reshape(layers, query_count, group_heads, HEAD_DIM)
            .transpose(0, 2, 1, 3)
            .reshape(pair_count, query_count, HEAD_DIM)
        )

    query_heads = split_heads(query_all)
    grad_heads = split_heads(grad_all)
    delta_heads = delta_all.transpose(0, 2, 1).reshape(pair_count, query_count)
    key_heads = key_block.reshape(key_count, group_heads, HEAD_DIM).transpose(1, 0, 2)
    value_heads = value_block.reshape(key_count, group_heads, HEAD_DIM).transpose(1, 0, 2)
    head_ids = jnp.arange(pair_count, dtype=jnp.int32) % group_heads
    ctx_index = lax.axis_index("ctx")
    key_pos = block_order[ctx_index] * key_count + jnp.arange(key_count, dtype=jnp.int32)
    query_pos = key_total - query_count + jnp.arange(query_count, dtype=jnp.int32)
    visible = key_pos[None, :] <= query_pos[:, None]

    def masked_scores(query_head, head_index):
        scores = (
            jnp.dot(query_head, key_heads[head_index].T, preferred_element_type=jnp.float32)
            * scaling
        )
        return jnp.where(visible, scores, masked_score)

    def local_stats(packed):
        query_head, head_index = packed
        scores = masked_scores(query_head, head_index)
        row_max = jnp.max(scores, axis=1)
        row_sum = jnp.sum(jnp.where(visible, jnp.exp(scores - row_max[:, None]), 0.0), axis=1)
        return (row_max, row_sum)

    row_max, row_sum = lax.map(local_stats, (query_heads, head_ids))
    peak_max = lax.pmax(row_max.astype(jnp.bfloat16), "ctx").astype(row_max.dtype)
    row_sum = lax.psum(row_sum * jnp.exp(row_max - peak_max), "ctx")
    row_max = peak_max
    log_total = row_max + jnp.log(row_sum)

    def gradients(packed):
        query_head, grad_head, delta_head, total_head, head_index = packed
        scores = masked_scores(query_head, head_index)
        prob = jnp.where(visible, jnp.exp(scores - total_head[:, None]), 0.0)
        prob_b = prob.astype(jnp.bfloat16)
        value_grad = jnp.dot(prob_b.T, grad_head, preferred_element_type=jnp.float32)
        prob_grad = jnp.dot(
            grad_head, value_heads[head_index].T, preferred_element_type=jnp.float32
        )
        score_grad = (prob * (prob_grad - delta_head[:, None]) * scaling).astype(jnp.bfloat16)
        query_grad = jnp.dot(score_grad, key_heads[head_index], preferred_element_type=jnp.float32)
        key_grad = jnp.dot(score_grad.T, query_head, preferred_element_type=jnp.float32)
        return (query_grad, key_grad, value_grad)

    query_grad, key_grad, value_grad = lax.map(
        gradients, (query_heads, grad_heads, delta_heads, log_total, head_ids)
    )
    query_layout = (
        query_grad.reshape(layers, group_heads, query_count, HEAD_DIM)
        .transpose(0, 2, 1, 3)
        .reshape(layers, query_count, group_heads * HEAD_DIM)
    )
    query_rows_sum = lax.psum_scatter(query_layout, "ctx", scatter_dimension=1, tiled=True)
    key_sum = (
        key_grad.reshape(layers, group_heads, key_count, HEAD_DIM)
        .sum(axis=0)
        .transpose(1, 0, 2)
        .reshape(key_count, group_heads * HEAD_DIM)
    )
    value_sum = (
        value_grad.reshape(layers, group_heads, key_count, HEAD_DIM)
        .sum(axis=0)
        .transpose(1, 0, 2)
        .reshape(key_count, group_heads * HEAD_DIM)
    )
    grad_queries = query_rows_sum.astype(jnp.bfloat16)
    key_part, value_part = (
        lax.psum_scatter(
            key_sum.astype(jnp.bfloat16), "section", scatter_dimension=1, tiled=True
        ).astype(jnp.float32),
        lax.psum_scatter(
            value_sum.astype(jnp.bfloat16), "section", scatter_dimension=1, tiled=True
        ).astype(jnp.float32),
    )
    grad_keys = key_part.astype(jnp.bfloat16)
    grad_values = value_part.astype(jnp.bfloat16)
    return (grad_queries, grad_keys, grad_values)


def solution(mesh):
    in_specs = (
        P(),
        P("section", "ctx", None),
        P("ctx", "section"),
        P("ctx", "section"),
        P("section", "ctx", None),
        P("section", "ctx", None),
    )
    out_specs = (P("section", "ctx", None), P("ctx", "section"), P("ctx", "section"))
    return jax.shard_map(local, mesh=mesh, in_specs=in_specs, out_specs=out_specs, check_vma=False)
```

profile of v0, /device:TPU:1, one launch (start us, length us, event | category | flops | bytes accessed | tf_op | source)
XLA Modules:
  0.0 1952.7 jit_solution(12765370029345223563)
XLA Ops:
  11.8 9.9 all_gather.16
  23.0 8.0 all_gather.18
  31.2 157.5 %all-gather = f32[512,20]{1,0:T(8,128)S(1)} all-gather(f32[8,20]{1,0:T(8,128)S(1)} %copy.52), channel_id=2, replica_groups=mesh['section'=4,'ctx'=64] {'ctx'}, dimensions={0}, use_global_device_ids=true | all-gather | bytes 41600 | tf_op jit(solution)/shard_map/all_gather | solution.py:34
  188.8 3.0 copy.46
  191.8 2.6 copy.53
  194.4 78.3 %while.28 = (s32[]{:T(128)}, f32[20,512]{1,0:T(8,128)S(1)}, f32[20,512]{1,0:T(8,128)S(1)}, bf16[20,512,128]{2,1,0:T(8,128)(2,1)}, s32[20]{0:T(128)S(1)}, /*index...) while((s32[]{:T(128)}, f32[20,512]{1,0:T(8,128)S(1)}, ...), condition=%wide.region_4.5_spmd.clone, body=%wide.region_1.4_spmd.clone.sunk | while | flops 17300484 | bytes 708263 | solution.py:68
  272.7 296.8 %pmax.7 = bf16[20,512]{1,0:T(8,128)(2,1)S(1)} all-reduce(bf16[20,512]{1,0:T(8,128)(2,1)S(1)} %convert_element_type.43), channel_id=1, replica_groups=mesh['section'=4,'ctx'=64] {'ctx'}, use_global_device_ids=true, to_apply=%region_5.6 | all-reduce | flops 10240 | bytes 40960 | tf_op jit(solution)/shard_map/pmax | solution.py:69
  569.5 296.7 %psum.7 = f32[20,512]{1,0:T(8,128)S(1)} all-reduce(f32[20,512]{1,0:T(8,128)S(1)} %fusion.42), channel_id=1, replica_groups=mesh['section'=4,'ctx'=64] {'ctx'}, use_global_device_ids=true, to_apply=%region_6.7 | all-reduce | flops 10240 | bytes 81920 | tf_op jit(solution)/shard_map/psum | solution.py:70
  866.3 3.0 copy.50
  869.3 163.1 %while.29 = (s32[]{:T(128)}, f32[20,512,128]{1,2,0:T(8,128)}, bf16[20,128,128]{1,2,0:T(8,128)(2,1)}, bf16[20,128,128]{1,2,0:T(8,128)(2,1)}, bf16[20,512,128]{2,1...) while((s32[]{:T(128)}, f32[20,512,128]{1,2,0:T(8,128)}, ...), condition=%wide.region_8.9_spmd.clone, body=%wide.region_7.8_spmd.clone.sunk | while | flops 84541440 | bytes 2213591 | solution.py:88
  874.9 1.7 fusion.78
  883.1 1.7 fusion.78
  891.2 1.8 fusion.78
  897.7 1.7 fusion.77
  899.4 1.7 fusion.78
  905.9 1.7 fusion.77
  907.6 1.7 fusion.78
  914.0 1.7 fusion.77
  915.7 1.7 fusion.78
  923.9 1.7 fusion.78
  930.3 1.7 fusion.77
  932.0 1.7 fusion.78
  938.5 1.7 fusion.77
  940.2 1.7 fusion.78
  946.7 1.7 fusion.77
  948.4 1.7 fusion.78
  956.5 1.7 fusion.78
  963.0 1.7 fusion.77
  964.7 1.7 fusion.78
  971.1 1.7 fusion.77
  972.8 1.7 fusion.78
  979.3 1.7 fusion.77
  981.0 1.7 fusion.78
  989.1 1.7 fusion.78
  995.6 1.7 fusion.77
  997.3 1.7 fusion.78
  1005.4 1.7 fusion.78
  1013.6 1.7 fusion.78
  1020.0 1.7 fusion.77
  1021.7 1.7 fusion.78
  1028.2 1.7 fusion.77
  1029.9 1.7 fusion.78
  1033.7 11.7 copy.59
  1045.4 777.4 %all-reduce.2 = bf16[1,512,2560]{2,0,1:T(2,128)(2,1)} all-reduce(f32[1,512,2560]{2,0,1:T(1,128)} %copy.59), channel_id=3, replica_groups=mesh['section'=4,'ctx'=64] {'ctx'}, use_global_device_ids=true, to_apply=%region_9.10.clone | all-reduce | flops 1310720 | bytes 7864320
  1824.4 61.0 %reduce-scatter.3.cloned.1.call-done = bf16[128,640]{0,1:T(8,128)(2,1)} async-done(((bf16[128,2560]{0,1:T(8,128)(2,1)}), bf16[128,640]{0,1:T(8,128)(2,1)}) %reduce-scatter.3.cloned.1.call-update) | async-done | bytes 163856 | tf_op jit(solution)/shard_map/reduce_scatter | solution.py:111
  1885.4 1.7 copy.63
  1887.1 57.3 %reduce-scatter.5.cloned.1.call-done = bf16[128,640]{0,1:T(8,128)(2,1)} async-done(((bf16[128,2560]{0,1:T(8,128)(2,1)}), bf16[128,640]{0,1:T(8,128)(2,1)}) %reduce-scatter.5.cloned.1.call-update) | async-done | bytes 163856 | tf_op jit(solution)/shard_map/reduce_scatter | solution.py:114
  1944.4 1.7 copy.64
  (248 shorter events, 114.9 us)
Async XLA Ops:
  7.2 23.8 %copy-start.1 = (bf16[1,8,2560]{2,1,0:T(8,128)(2,1)S(1)}, bf16[1,8,2560]{2,1,0:T(8,128)(2,1)}, u32[]{:S(2)}) copy-start(bf16[1,8,2560]{2,1,0:T(8,128)(2,1)} %param.15) | copy-start | bytes 122884
  7.2 15.7 copy-start
  7.2 23.8 %copy-start.2 = (bf16[1,8,2560]{2,1,0:T(8,128)(2,1)S(1)}, bf16[1,8,2560]{2,1,0:T(8,128)(2,1)}, u32[]{:S(2)}) copy-start(bf16[1,8,2560]{2,1,0:T(8,128)(2,1)} %param.14) | copy-start | bytes 122884
  7.2 181.6 %all-gather.4.cloned.1.call-start = ((), (), s32[]{:S(2)}) async-start(), calls=%async_computation.2 | async-start | bytes 2662400 | tf_op jit(solution)/shard_map/all_gather | solution.py:31
  7.9 858.4 %all-gather.6.cloned.1.call-start = ((), (), s32[]{:S(2)}) async-start(), calls=%async_computation.3 | async-start | bytes 2662400 | tf_op jit(solution)/shard_map/all_gather | solution.py:32
  8.7 1876.7 %reduce-scatter.3.cloned.1.call-start = ((), (), s32[]{:S(2)}) async-start(), calls=%async_computation.4 | async-start | bytes 819200 | tf_op jit(solution)/shard_map/reduce_scatter | solution.py:111
  869.3 163.2 %copy-start.3 = (u32[256]{0:T(256)S(1)}, u32[256]{0:T(256)}, u32[]{:S(2)}) copy-start(u32[256]{0:T(256)} %constant.79) | copy-start | bytes 3076
  1032.4 912.0 %reduce-scatter.5.cloned.1.call-start = ((), (), s32[]{:S(2)}) async-start(), calls=%async_computation.5 | async-start | bytes 819200 | tf_op jit(solution)/shard_map/reduce_scatter | solution.py:114
Sparse Core Ops, SparseCore 0:
  11.5 121.2 all-gather.3
  136.4 117.5 all-gather.5
  1032.5 852.8 reduce-scatter.2
  1887.8 56.5 reduce-scatter.4
where the time goes:
time: 1980 us; the launch traced here: 1950 us
  blocking collectives  1550 us (78%)
  matrix products  134 us (7%)
  waiting for transfers between devices  120 us (6%)
  loops' own time  79 us (4%)
  local copies, waits for them, and re-layouts  55.8 us (3%)
    unnamed x1, blocking collectives  777 us
    pmax x1, blocking collectives, local(): lax.pmax(row_max.astype(jnp.bfloat16), 'ctx').astype(row_max.dtype)  297 us
    psum x1, blocking collectives, local(): row_sum = lax.psum(row_sum * jnp.exp(row_max - peak_max), 'ctx')  297 us
    all_gather x1, blocking collectives, local(): delta_all = lax.all_gather(delta_part, 'ctx', axis=1, tiled=True)  157 us
    reduce_scatter x1, waiting for transfers between devices, local(): lax.psum_scatter(key_sum.astype(jnp.bfloat16), 'section', scatter_dimensi...  61 us
    reduce_scatter x1, waiting for transfers between devices, local(): lax.psum_scatter(value_sum.astype(jnp.bfloat16), 'section', scatter_dimen...  57.3 us
    dot_general x40, matrix products, masked_scores(): jnp.dot(query_head, key_heads[head_index].T, preferred_element_type=jnp.f...  45.1 us
  transfers between devices with their start and end apart: 4, of which 2 were waited for; matrix products, arithmetic and copies ran while one was open for 3% of the time, Pallas kernels for 0%

commit v1 on v0

v1 whole, which is shorter than its diff:
```python
import jax
import jax.numpy as jnp
from jax import lax
from jax.experimental import pallas as pl
from jax.experimental.pallas import tpu as pltpu
from jax.sharding import PartitionSpec as P

MESH = pl.DeviceIdType.MESH
F32 = jnp.float32
BF16 = jnp.bfloat16

NS, NY, NX, NZ = 4, 4, 2, 8
HG, HD, GF = 5, 128, 640
KR = 128
KV = NY * KR
QR = 8
NB = NX * NY
ZR = NB * QR
QW = NZ * ZR
SCALE = HD ** -0.5
MASKED = -1e30
RT = 128


def nt(a, b):
    return lax.dot_general(a, b, (((1,), (1,)), ((), ())), preferred_element_type=F32)


def tn(a, b):
    return lax.dot_general(a, b, (((0,), (0,)), ((), ())), preferred_element_type=F32)


def nn(a, b):
    return lax.dot_general(a, b, (((1,), (0,)), ((), ())), preferred_element_type=F32)


def kernel(order, q_in, do_in, o_in, k_in, v_in, dq_out, dk_out, dv_out,
           pk, pdel, p1, p1d, g, gd0, gd, kv, q3, do3, delc, pu, ds0, m3, lse3, c3, ls, lsx, lz,
           dqa, dkv, sqr, sql, rqr, rql, kvs, kvr, tb, p8, p9s, p9,
           s1, r1, s1d, r1d, s2, r2, s2d, r2d, sz, rz, szd, rzd, sy, ry, sl, rl, sx, rx,
           sg, rg, sk, rk, s8, r8, s9, r9):
    s = lax.axis_index("section")
    c = lax.axis_index("ctx")
    y = c // (NX * NZ)
    xh = (c // NZ) % NX
    z = c % NZ

    def dev(s_, y_, x_, z_):
        return (s_, (y_ * NX + x_) * NZ + z_)

    def rc(src, dst, ssem, rsem, to):
        return pltpu.make_async_remote_copy(
            src_ref=src, dst_ref=dst, send_sem=ssem, recv_sem=rsem,
            device_id=to, device_id_type=MESH)

    def up(v, n, mod):
        return (v + n) % mod

    def dn(v, n, mod):
        return (v + mod - n) % mod

    me = (s, c)
    others = [(j, k) for j in range(NY) for k in range(NX) if (j, k) != (0, 0)]

    bar = pltpu.get_barrier_semaphore()
    partners = [dev(up(s, j, NS), y, xh, z) for j in range(1, NS)]
    partners += [dev(s, up(y, j, NY), up(xh, k, NX), z) for j, k in others]
    partners += [dev(s, y, xh, up(z, j, NZ)) for j in range(1, NZ)]
    for p in partners:
        pl.semaphore_signal(bar, inc=1, device_id=p, device_id_type=MESH)

    lane = lax.broadcasted_iota(jnp.int32, (QR, 128), 1)
    for t in range(NS):
        cols = slice(t * GF, (t + 1) * GF)
        qf = q_in[0, :, cols].astype(F32)
        df = do_in[0, :, cols].astype(F32)
        of = o_in[0, :, cols].astype(F32)
        pk[t] = jnp.concatenate([qf, df], axis=0).astype(BF16)
        prod = df * of
        tile = jnp.zeros((QR, 128), F32)
        for h in range(HG):
            d = jnp.sum(prod[:, h * HD:(h + 1) * HD], axis=1, keepdims=True)
            tile = jnp.where(lane == h, d, tile)
        pdel[t] = tile
    for h in range(HG):
        kv[y, 0, h] = k_in[:, h * HD:(h + 1) * HD]
        kv[y, 1, h] = v_in[:, h * HD:(h + 1) * HD]

    pl.semaphore_wait(bar, len(partners))

    sends = []

    def go(cp):
        cp.start()
        sends.append(cp)

    for j in range(1, NS):
        t = up(s, j, NS)
        go(rc(pk.at[t], p1.at[s], s1.at[j], r1.at[j], (t, c)))
        go(rc(pdel.at[t], p1d.at[s], s1d.at[j], r1d.at[j], (t, c)))

    yr, yl = up(y, 1, NY), dn(y, 1, NY)
    y2 = up(y, 2, NY)
    dyr, dyl = dev(s, yr, xh, z), dev(s, yl, xh, z)
    for a in range(2):
        go(rc(kv.at[y, a], kv.at[y, a], sy.at[0, a], ry.at[0, a], dyr))
        go(rc(kv.at[y, a], kv.at[y, a], sy.at[1, a], ry.at[1, a], dyl))

    p1[s] = pk[s]
    p1d[s] = pdel[s]
    for j in range(1, NS):
        f = dn(s, j, NS)
        rc(p1.at[f], p1.at[f], s1.at[j], r1.at[j], me).wait_recv()
        rc(p1d.at[f], p1d.at[f], s1d.at[j], r1d.at[j], me).wait_recv()

    mine = xh * NY + y
    for j, k in others:
        ty, tx = up(y, j, NY), up(xh, k, NX)
        to = dev(s, ty, tx, z)
        go(rc(p1.at[ty], g.at[z, mine], s2.at[j, k], r2.at[j, k], to))
        go(rc(p1d.at[ty], gd0.at[mine], s2d.at[j, k], r2d.at[j, k], to))
    g[z, mine] = p1[y]
    gd0[mine] = p1d[y]
    for j, k in others:
        f = dn(xh, k, NX) * NY + dn(y, j, NY)
        rc(g.at[z, f], g.at[z, f], s2.at[j, k], r2.at[j, k], me).wait_recv()
        rc(gd0.at[f], gd0.at[f], s2d.at[j, k], r2d.at[j, k], me).wait_recv()
    tile = gd0[0]
    for b in range(1, NB):
        tile = tile + pltpu.roll(gd0[b], b * QR, 1)
    gd[z] = tile

    zr, zl = up(z, 1, NZ), dn(z, 1, NZ)
    dzr, dzl = dev(s, y, xh, zr), dev(s, y, xh, zl)
    half = NB // 2

    def zmsg(d, t, hf):
        src = dn(z, t - 1, NZ) if d == 0 else up(z, t - 1, NZ)
        ref = g.at[src, pl.ds(hf * half, half)]
        return rc(ref, ref, sz.at[d, t - 1, hf], rz.at[d, t - 1, hf], dzr if d == 0 else dzl)

    def zin(d, t, hf):
        src = dn(z, t, NZ) if d == 0 else up(z, t, NZ)
        ref = g.at[src, pl.ds(hf * half, half)]
        return rc(ref, ref, sz.at[d, t - 1, hf], rz.at[d, t - 1, hf], me)

    def zdmsg(d, t):
        src = dn(z, t - 1, NZ) if d == 0 else up(z, t - 1, NZ)
        return rc(gd.at[src], gd.at[src], szd.at[d, t - 1], rzd.at[d, t - 1], dzr if d == 0 else dzl)

    def zdin(d, t):
        src = dn(z, t, NZ) if d == 0 else up(z, t, NZ)
        return rc(gd.at[src], gd.at[src], szd.at[d, t - 1], rzd.at[d, t - 1], me)

    def unpack(zc):
        blk = g[zc].astype(F32).reshape(NB, 2, QR, GF)
        qc = blk[:, 0].reshape(ZR, GF).astype(BF16)
        dc = blk[:, 1].reshape(ZR, GF).astype(BF16)
        rows = pl.ds(pl.multiple_of(zc * ZR, ZR), ZR)
        for h in range(HG):
            q3[h, rows] = qc[:, h * HD:(h + 1) * HD]
            do3[h, rows] = dc[:, h * HD:(h + 1) * HD]
        tile = gd[zc]
        for b in range(NB):
            piece = tile if b == 0 else pltpu.roll(tile, 128 - b * QR, 1)
            delc[pl.ds(pl.multiple_of(zc * ZR + b * QR, QR), QR)] = piece

    for t in range(1, NZ // 2 + 1):
        last = t == NZ // 2
        for hf in range(2):
            for d in range(2):
                if last and hf != d:
                    continue
                if t > 1:
                    zin(d, t - 1, hf).wait_recv()
                go(zmsg(d, t, hf))
        if last:
            for d in range(2):
                zin(d, t - 1, 1 - d).wait_recv()
        for d in range(2):
            if t > 1:
                zdin(d, t - 1).wait_recv()
            if not (last and d == 1):
                go(zdmsg(d, t))
        if t == 1:
            rc(kv.at[yl, 0], kv.at[yl, 0], sy.at[0, 0], ry.at[0, 0], me).wait_recv()
            go(rc(kv.at[yl, 0], kv.at[yl, 0], sy.at[2, 0], ry.at[2, 0], dyr))
            rc(kv.at[yr, 1], kv.at[yr, 1], sy.at[1, 1], ry.at[1, 1], me).wait_recv()
            go(rc(kv.at[yr, 1], kv.at[yr, 1], sy.at[2, 1], ry.at[2, 1], dyl))
            unpack(z)
        else:
            unpack(dn(z, t - 1, NZ))
            unpack(up(z, t - 1, NZ))
    zin(0, NZ // 2, 0).wait_recv()
    zin(1, NZ // 2, 1).wait_recv()
    zdin(0, NZ // 2).wait_recv()
    unpack(up(z, NZ // 2, NZ))
    rc(kv.at[yl, 1], kv.at[yl, 1], sy.at[0, 1], ry.at[0, 1], me).wait_recv()
    rc(kv.at[yr, 0], kv.at[yr, 0], sy.at[1, 0], ry.at[1, 0], me).wait_recv()
    rc(kv.at[y2, 0], kv.at[y2, 0], sy.at[2, 0], ry.at[2, 0], me).wait_recv()
    rc(kv.at[y2, 1], kv.at[y2, 1], sy.at[2, 1], ry.at[2, 1], me).wait_recv()

    kcol = lax.broadcasted_iota(jnp.int32, (1, KV), 1)
    kblk = kcol // KR
    base = jnp.zeros((1, KV), jnp.int32)
    for b in range(NY):
        base = jnp.where(kblk == b, order[(b * NX + xh) * NZ + z], base)
    kpos = base * KR + kcol % KR
    first = NY * NX * NZ * KR - QW

    def qpos(rt):
        r = lax.broadcasted_iota(jnp.int32, (RT, 1), 0) + rt * RT
        rz_, rx_, ry_, rr = r // ZR, (r // (NY * QR)) % NX, (r // QR) % NY, r % QR
        return first + ((ry_ * NX + rx_) * NZ + rz_) * QR + rr

    NR = QW // RT

    def scores(h, _):
        kh = kv[:, 0, h].reshape(KV, HD)
        for rt in range(NR):
            rows = slice(rt * RT, (rt + 1) * RT)
            sc = nt(q3[h, rows], kh) * SCALE
            sc = jnp.where(kpos <= qpos(rt), sc, MASKED)
            m = jnp.max(sc, axis=1, keepdims=True)
            p = jnp.exp(sc - m)
            l = jnp.sum(p, axis=1, keepdims=True)
            pu[h, rows] = p
            m3[h, rows] = jnp.broadcast_to(m, (RT, 128))
            lse3[h, rows] = jnp.broadcast_to(m + jnp.log(l), (RT, 128))
        return 0

    lax.fori_loop(0, HG, scores, 0)

    lane2 = lax.broadcasted_iota(jnp.int32, (RT, 128), 1)
    for rt in range(NR):
        rows = slice(rt * RT, (rt + 1) * RT)
        st = jnp.zeros((RT, 128), F32)
        for h in range(HG):
            st = jnp.where(lane2 == h, lse3[h, rows], st)
        ls[:, rows] = st.T[:8]
    dx = dev(s, y, up(xh, 1, NX), z)
    cpx = rc(ls, lsx, sx.at[0], rx.at[0], dx)
    go(cpx)

    def dprob(h, _):
        vh = kv[:, 1, h].reshape(KV, HD)
        for rt in range(NR):
            rows = slice(rt * RT, (rt + 1) * RT)
            dl = jnp.zeros((RT, 128), F32)
            dl = jnp.sum(jnp.where(lane2 == h, delc[rows], dl), axis=1, keepdims=True)
            dp = nt(do3[h, rows], vh)
            ds0[h, rows] = pu[h, rows] * (dp - dl) * SCALE
        return 0

    cpx.wait_recv()
    a, b = ls[...], lsx[...]
    mx = jnp.maximum(a, b)
    lz[z] = mx + jnp.log(jnp.exp(a - mx) + jnp.exp(b - mx))
    for j in range(1, NZ):
        go(rc(lz.at[z], lz.at[z], sl.at[j], rl.at[j], dev(s, y, xh, up(z, j, NZ))))
    lax.fori_loop(0, HG, dprob, 0)
    for j in range(1, NZ):
        f = dn(z, j, NZ)
        rc(lz.at[f], lz.at[f], sl.at[j], rl.at[j], me).wait_recv()
    mx = lz[0]
    for j in range(1, NZ):
        mx = jnp.maximum(mx, lz[j])
    tot = jnp.exp(lz[0] - mx)
    for j in range(1, NZ):
        tot = tot + jnp.exp(lz[j] - mx)
    lt = mx + jnp.log(tot)
    for rt in range(NR):
        rows = slice(rt * RT, (rt + 1) * RT)
        tt = jnp.concatenate([lt[:, rows], jnp.zeros((120, RT), F32)], axis=0).T
        for h in range(HG):
            cc = jnp.exp(m3[h, rows] - jnp.broadcast_to(tt[:, h:h + 1], (RT, 128)))
            c3[h, rows] = cc

    def grads(h, _):
        kh = kv[:, 0, h].reshape(KV, HD)
        dkt = jnp.zeros((HD, KV), F32)
        dvt = jnp.zeros((HD, KV), F32)
        cols = pl.ds(pl.multiple_of(h * HD, HD), HD)
        for rt in range(NR):
            rows = slice(rt * RT, (rt + 1) * RT)
            cc = c3[h, rows][:, :1]
            pb = (pu[h, rows] * cc).astype(BF16)
            db = (ds0[h, rows] * cc).astype(BF16)
            dvt = dvt + tn(do3[h, rows], pb)
            dkt = dkt + tn(q3[h, rows], db)
            dq = nn(db, kh)
            for i in range(RT // ZR):
                dqa[rt * (RT // ZR) + i, :, cols] = dq[i * ZR:(i + 1) * ZR]
        for b in range(NY):
            dkv[b, 0, h] = dkt[:, b * KR:(b + 1) * KR].T
            dkv[b, 1, h] = dvt[:, b * KR:(b + 1) * KR].T
        return 0

    lax.fori_loop(0, HG, grads, 0)

    kvs[0, 0] = dkv[y2, 0].astype(BF16)
    go(rc(kvs.at[0, 0], kvr.at[0, 0], sk.at[0, 0], rk.at[0, 0], dyr))
    kvs[0, 1] = dkv[y2, 1].astype(BF16)
    go(rc(kvs.at[0, 1], kvr.at[0, 1], sk.at[0, 1], rk.at[0, 1], dyl))
    kvs[1, 1] = dkv[yr, 1].astype(BF16)
    go(rc(kvs.at[1, 1], kvr.at[1, 1], sk.at[1, 1], rk.at[1, 1], dyr))
    kvs[2, 0] = dkv[yl, 0].astype(BF16)
    go(rc(kvs.at[2, 0], kvr.at[2, 0], sk.at[2, 0], rk.at[2, 0], dyl))

    NH = NZ // 2
    HR = ZR // 2

    def qmsg(d, t):
        snd, rcv = (sqr, rqr) if d == 0 else (sql, rql)
        a_, b_ = snd.at[t - 1], rcv.at[t - 1]
        if t == NH:
            part = pl.ds(d * HR, HR)
            a_, b_ = snd.at[t - 1, part], rcv.at[t - 1, part]
        return rc(a_, b_, sg.at[d, t - 1], rg.at[d, t - 1], dzr if d == 0 else dzl)

    for t in range(NH, 0, -1):
        for d in range(2):
            snd, rcv = (sqr, rqr) if d == 0 else (sql, rql)
            dest = up(z, t, NZ) if d == 0 else dn(z, t, NZ)
            part = slice(d * HR, (d + 1) * HR)
            if t == NH:
                snd[t - 1, part] = dqa[dest, part].astype(BF16)
            else:
                qmsg(d, t + 1).wait_recv()
                if t == NH - 1:
                    rest = slice((1 - d) * HR, (2 - d) * HR)
                    snd[t - 1, rest] = dqa[dest, rest].astype(BF16)
                    snd[t - 1, part] = (dqa[dest, part] + rcv[t, part].astype(F32)).astype(BF16)
                else:
                    snd[t - 1] = (dqa[dest] + rcv[t].astype(F32)).astype(BF16)
            go(qmsg(d, t))
        if t == NH - 1:
            rc(kvr.at[0, 0], kvr.at[0, 0], sk.at[0, 0], rk.at[0, 0], me).wait_recv()
            kvs[1, 0] = (dkv[yr, 0] + kvr[0, 0].astype(F32)).astype(BF16)
            go(rc(kvs.at[1, 0], kvr.at[1, 0], sk.at[1, 0], rk.at[1, 0], dyr))
            rc(kvr.at[0, 1], kvr.at[0, 1], sk.at[0, 1], rk.at[0, 1], me).wait_recv()
            kvs[2, 1] = (dkv[yl, 1] + kvr[0, 1].astype(F32)).astype(BF16)
            go(rc(kvs.at[2, 1], kvr.at[2, 1], sk.at[2, 1], rk.at[2, 1], dyl))
    qmsg(0, 1).wait_recv()
    qmsg(1, 1).wait_recv()
    tb[...] = (dqa[z] + rqr[0].astype(F32) + rql[0].astype(F32)).reshape(NB, QR, GF)

    for j, k in others:
        ty, tx = up(y, j, NY), up(xh, k, NX)
        go(rc(tb.at[tx * NY + ty], p8.at[xh, y], s8.at[j, k], r8.at[j, k], dev(s, ty, tx, z)))
    p8[xh, y] = tb[mine]
    for j, k in others:
        fx, fy = dn(xh, k, NX), dn(y, j, NY)
        rc(p8.at[fx, fy], p8.at[fx, fy], s8.at[j, k], r8.at[j, k], me).wait_recv()
    p9s[...] = p8[0] + p8[1]
    for j in range(1, NS):
        t = up(s, j, NS)
        go(rc(p9s.at[t], p9.at[s], s9.at[j], r9.at[j], (t, c)))
    p9[s] = p9s[s]
    for j in range(1, NS):
        f = dn(s, j, NS)
        rc(p9.at[f], p9.at[f], s9.at[j], r9.at[j], me).wait_recv()
    for t in range(NS):
        dq_out[0, :, t * GF:(t + 1) * GF] = p9[t].astype(BF16)

    for a in range(2):
        rc(kvr.at[1, a], kvr.at[1, a], sk.at[1, a], rk.at[1, a], me).wait_recv()
        rc(kvr.at[2, a], kvr.at[2, a], sk.at[2, a], rk.at[2, a], me).wait_recv()
        out = dk_out if a == 0 else dv_out
        for h in range(HG):
            acc = dkv[y, a, h] + kvr[1, a, h].astype(F32) + kvr[2, a, h].astype(F32)
            out[:, h * HD:(h + 1) * HD] = acc.astype(BF16)
    for cp in sends:
        cp.wait_send()


def local(block_order, queries, cache_keys, cache_values, attention_out, output_grad):
    dma = pltpu.SemaphoreType.DMA
    vm = pltpu.VMEM
    scratch = [
        vm((NS, 16, GF), BF16), vm((NS, QR, 128), F32), vm((NS, 16, GF), BF16), vm((NS, QR, 128), F32),
        vm((NZ, NB, 16, GF), BF16), vm((NB, QR, 128), F32), vm((NZ, QR, 128), F32),
        vm((NY, 2, HG, KR, HD), BF16), vm((HG, QW, HD), BF16), vm((HG, QW, HD), BF16), vm((QW, 128), F32),
        vm((HG, QW, KV), F32), vm((HG, QW, KV), F32),
        vm((HG, QW, 128), F32), vm((HG, QW, 128), F32), vm((HG, QW, 128), F32),
        vm((8, QW), F32), vm((8, QW), F32), vm((NZ, 8, QW), F32),
        vm((NZ, ZR, GF), F32), vm((NY, 2, HG, KR, HD), F32),
        vm((4, ZR, GF), BF16), vm((4, ZR, GF), BF16), vm((4, ZR, GF), BF16), vm((4, ZR, GF), BF16),
        vm((3, 2, HG, KR, HD), BF16), vm((3, 2, HG, KR, HD), BF16),
        vm((NB, QR, GF), F32), vm((NX, NY, QR, GF), F32), vm((NS, QR, GF), F32), vm((NS, QR, GF), F32),
        dma((NS,)), dma((NS,)), dma((NS,)), dma((NS,)),
        dma((NY, NX)), dma((NY, NX)), dma((NY, NX)), dma((NY, NX)),
        dma((2, 4, 2)), dma((2, 4, 2)), dma((2, 4)), dma((2, 4)),
        dma((3, 2)), dma((3, 2)), dma((NZ,)), dma((NZ,)), dma((1,)), dma((1,)),
        dma((2, 4)), dma((2, 4)), dma((3, 2)), dma((3, 2)),
        dma((NY, NX)), dma((NY, NX)), dma((NS,)), dma((NS,)),
    ]
    vspec = pl.BlockSpec(memory_space=pltpu.VMEM)
    dq, dk, dv = pl.pallas_call(
        kernel,
        out_shape=(
            jax.ShapeDtypeStruct((1, QR, NS * GF), BF16),
            jax.ShapeDtypeStruct((KR, GF), BF16),
            jax.ShapeDtypeStruct((KR, GF), BF16),
        ),
        in_specs=[pl.BlockSpec(memory_space=pltpu.SMEM)] + [vspec] * 5,
        out_specs=(vspec, vspec, vspec),
        scratch_shapes=scratch,
        compiler_params=pltpu.CompilerParams(
            collective_id=0, has_side_effects=True, vmem_limit_bytes=56 << 20),
    )(block_order, queries, output_grad, attention_out, cache_keys, cache_values)
    return dq, dk, dv


def solution(mesh):
    in_specs = (
        P(),
        P("section", "ctx", None),
        P("ctx", "section"),
        P("ctx", "section"),
        P("section", "ctx", None),
        P("section", "ctx", None),
    )
    out_specs = (P("section", "ctx", None), P("ctx", "section"), P("ctx", "section"))
    return jax.shard_map(local, mesh=mesh, in_specs=in_specs, out_specs=out_specs, check_vma=False)
```

time: 1980 us -> 87.9 us (0.04); the launches traced: 1950 us -> 87.8 us
  blocking collectives: 1550 us -> 0 us
  matrix products: 134 us -> 0 us
  waiting for transfers between devices: 120 us -> 0 us
  Pallas kernels: 0 us -> 83.4 us
  loops' own time: 79 us -> 0 us
  local copies, waits for them, and re-layouts: 55.8 us -> 3.7 us
    unnamed x1 -> x0, blocking collectives: 777 us -> none
    pmax x1 -> x0, blocking collectives: 297 us -> none  [local(): lax.pmax(row_max.astype(jnp.bfloat16), 'ctx').astype(row_max.dtype)]
    psum x1 -> x0, blocking collectives: 297 us -> none  [local(): row_sum = lax.psum(row_sum * jnp.exp(row_max - peak_max), 'ctx')]
    all_gather x3 -> x0, blocking collectives: 175 us -> none  [the longest x1 157 us: local(): delta_all = lax.all_gather(delta_part, 'ctx', axis=1, tiled=True)]
    dot_general x120 -> x0, matrix products: 134 us -> none  [the longest x40 45.1 us: masked_scores(): jnp.dot(query_head, key_heads[head_index].T, preferred_element_type=jnp.f...]
    reduce_scatter x2 -> x0, waiting for transfers between devices: 118 us -> none  [the longest x1 61 us: local(): lax.psum_scatter(key_sum.astype(jnp.bfloat16), 'section', scatter_dimensi...]
    pallas_call x0 -> x1, Pallas kernels: none -> 83.4 us  [local(): pl.pallas_call(kernel, out_shape=(jax.ShapeDtypeStruct((1, QR, NS * GF),...]
    another operation x2 -> x0, loops' own time: 79 us -> none  [the longest x1 39.6 us: local(): row_max, row_sum = lax.map(local_stats, (query_heads, head_ids))]
  transfers between devices with their start and end apart: 4 -> 0, of which waited for: 2 -> 0; matrix products, arithmetic and copies ran while one was open for 3% -> 0% of each run, Pallas kernels for 0% -> 0%
where the time goes in v1:
time: 87.9 us; the launch traced here: 87.8 us
  Pallas kernels  83.4 us (95%)
  local copies, waits for them, and re-layouts  3.7 us (4%)
    pallas_call x1, Pallas kernels, local(): pl.pallas_call(kernel, out_shape=(jax.ShapeDtypeStruct((1, QR, NS * GF),...  83.4 us
    unnamed x5, local copies, waits for them, and re-layouts  3.7 us

profile of v1, /device:TPU:1, one launch (start us, length us, event | category | flops | bytes accessed | tf_op | source)
XLA Modules:
  0.0 87.8 jit_solution(6264738854183795966)
XLA Ops:
  0.6 83.4 %shard_map.85 = (bf16[1,8,2560]{2,1,0:T(8,128)(2,1)}, bf16[128,640]{1,0:T(8,128)(2,1)}, bf16[128,640]{1,0:T(8,128)(2,1)}) custom-call(s32[64]{0:T(128)} %order.1, bf16[1,8,2560]{2,1,0:T(8,128)(2,1)} %q_in.1, bf16[1,8,2560]{2,1,0:T(8,128)(2,1)} %do_in.1, bf16[1,8,2560]{2,1,0:T(8,128)(2,1)} %o_in.1, bf16[128,640]{1,0:T(8,128)(2,1)} %k_in.1, bf16[128,640]{1,0:T(8,128)(2,1)} %v_in.1), custom_call_target="tpu_custom_call" | custom-call | tf_op jit(solution)/shard_map/pallas_call | solution.py:399
  84.1 1.4 %copy.12 = bf16[1,8,2560]{2,1,0:T(8,128)(2,1)} copy(bf16[1,8,2560]{2,1,0:T(8,128)(2,1)} %get-tuple-element.6) | data formatting | bytes 81920
  85.5 0.0 copy-start
  85.5 1.6 %copy.13 = bf16[128,640]{1,0:T(8,128)(2,1)} copy(bf16[128,640]{1,0:T(8,128)(2,1)} %get-tuple-element.7) | data formatting | bytes 327680
  87.1 0.0 copy-done
  87.1 0.7 copy.14
Async XLA Ops:
  85.5 1.6 %copy-start = (bf16[128,640]{1,0:T(8,128)(2,1)S(1)}, bf16[128,640]{1,0:T(8,128)(2,1)}, u32[]{:S(2)}) copy-start(bf16[128,640]{1,0:T(8,128)(2,1)} %get-tuple-element.8) | copy-start | bytes 491524

commit v2 on v0

v2 whole, which is shorter than its diff:
```python
import jax
import jax.numpy as jnp
from jax import lax
from jax.experimental import pallas as pl
from jax.experimental.pallas import tpu as pltpu
from jax.sharding import PartitionSpec as P

MESH = pl.DeviceIdType.MESH
F32 = jnp.float32
BF16 = jnp.bfloat16

NS, NY, NX, NZ = 4, 4, 2, 8
HG, HD, GF = 5, 128, 640
KR = 128
KV = NY * KR
QR = 8
NB = NX * NY
ZR = NB * QR
QW = NZ * ZR
NT = NZ // 2
SCALE = HD ** -0.5
MASKED = -1e30
RT = 128
NR = QW // RT
GROUPS = ((0, 1, 2), (3, 4))


def nt(a, b):
    return lax.dot_general(a, b, (((1,), (1,)), ((), ())), preferred_element_type=F32)


def tn(a, b):
    return lax.dot_general(a, b, (((0,), (0,)), ((), ())), preferred_element_type=F32)


def nn(a, b):
    return lax.dot_general(a, b, (((1,), (0,)), ((), ())), preferred_element_type=F32)


def kernel(order, q_in, do_in, o_in, k_in, v_in, dq_out, dk_out, dv_out,
           qv, dov, ov, kin, vin, pk, p1, g, gd, kv, q3, do3, delc, pu, ds0, m3, lse3, c3, lz,
           pbs, dbs, dqa, qs, qr, dkv, ks1, kr1, ks2, kr2, tb, p8,
           sin, s1, r1, sz, rz, szd, rzd, sy, ry, sf, rf, sl, rl, sg, rg, sk, rk, s8, r8):
    s = lax.axis_index("section")
    c = lax.axis_index("ctx")
    y = c // (NX * NZ)
    xh = (c // NZ) % NX
    z = c % NZ
    me = (s, c)
    own = s == y

    def dev(s_, y_, x_, z_):
        return (s_, (y_ * NX + x_) * NZ + z_)

    def rc(src, dst, ssem, rsem, to):
        return pltpu.make_async_remote_copy(
            src_ref=src, dst_ref=dst, send_sem=ssem, recv_sem=rsem,
            device_id=to, device_id_type=MESH)

    def arrived(dst, rsem):
        rc(dst, dst, rsem, rsem, me).wait_recv()

    def up(v, n, mod):
        return (v + n) % mod

    def dn(v, n, mod):
        return (v + mod - n) % mod

    sends = []

    def go(cp):
        cp.start()
        sends.append(cp)

    yr, yl, y2 = up(y, 1, NY), dn(y, 1, NY), up(y, 2, NY)
    bar = pltpu.get_barrier_semaphore()

    def greet(to):
        pl.semaphore_signal(bar, inc=1, device_id=to, device_id_type=MESH)

    count = 0
    for j in range(NZ):
        for k in range(NX):
            if (j, k) != (0, 0):
                greet(dev(s, y, up(xh, k, NX), up(z, j, NZ)))
                count += 1
    for t in (yr, yl):
        greet(dev(s, t, xh, z))
        count += 1
    for i in range(4):
        for k in range(NX):
            if (i, k) != (0, 0):
                greet(dev(up(s, i, NS), s, up(xh, k, NX), z))
                greet(dev(y, up(y, i, NY), up(xh, k, NX), z))
                count += 2

    @pl.when(jnp.logical_not(own))
    def _():
        greet(dev(s, s, xh, z))
        greet(dev(y, y, xh, z))

    loads = []
    for i, (a, b) in enumerate(((q_in, qv), (do_in, dov), (o_in, ov), (k_in, kin), (v_in, vin))):
        cp = pltpu.make_async_copy(a, b, sin.at[i])
        cp.start()
        loads.append(cp)
    for cp in loads:
        cp.wait()

    lane = lax.broadcasted_iota(jnp.int32, (QR, 128), 1)
    for t in range(NS):
        cols = slice(t * GF, (t + 1) * GF)
        qf = qv[0, :, cols].astype(F32)
        df = dov[0, :, cols].astype(F32)
        prod = df * ov[0, :, cols].astype(F32)
        both = jnp.concatenate([qf, df], axis=0).astype(BF16)
        tile = jnp.zeros((QR, 128), F32)
        for h in range(HG):
            pk[t, h] = both[:, h * HD:(h + 1) * HD]
            d = jnp.sum(prod[:, h * HD:(h + 1) * HD], axis=1, keepdims=True)
            tile = jnp.where(lane == h, d, tile)
        hi = tile.astype(BF16).astype(F32)
        mid = (tile - hi).astype(BF16).astype(F32)
        lo = tile - hi - mid
        pk[t, HG] = jnp.concatenate([hi + pltpu.roll(lo, QR, 1), mid], axis=0).astype(BF16)

    pl.semaphore_wait(bar, count + 2 - 2 * own.astype(jnp.int32))

    mine = xh * NY + y
    for k in range(NX):
        for i in range(NS):
            t = up(s, i, NS)
            cp = rc(pk.at[t], p1.at[mine], s1.at[i, k], r1.at[k, y], dev(t, s, up(xh, k, NX), z))
            if (i, k) == (0, 0):
                self_in = cp

                @pl.when(jnp.logical_not(own))
                def _():
                    cp.start()
            else:
                go(cp)

    @pl.when(own)
    def _():
        p1[mine] = pk[s]

    dyr, dyl = dev(s, yr, xh, z), dev(s, yl, xh, z)
    for h in range(HG):
        kv[y, h, 0] = kin[:, h * HD:(h + 1) * HD]
        kv[y, h, 1] = vin[:, h * HD:(h + 1) * HD]
        go(rc(kv.at[y, h], kv.at[y, h], sy.at[0, h], ry.at[0, h], dyr))
        go(rc(kv.at[y, h], kv.at[y, h], sy.at[1, h], ry.at[1, h], dyl))

    def kv_forward(h):
        arrived(kv.at[yl, h], ry.at[0, h])
        go(rc(kv.at[yl, h, 0], kv.at[yl, h, 0], sf.at[0, h], rf.at[0, h], dyr))
        arrived(kv.at[yr, h], ry.at[1, h])
        go(rc(kv.at[yr, h, 1], kv.at[yr, h, 1], sf.at[1, h], rf.at[1, h], dyl))

    def kv_ready(h):
        arrived(kv.at[y2, h, 0], rf.at[0, h])
        arrived(kv.at[y2, h, 1], rf.at[1, h])

    kcol = lax.broadcasted_iota(jnp.int32, (1, KV), 1)
    kblk = kcol // KR
    base = jnp.zeros((1, KV), jnp.int32)
    for b in range(NY):
        base = jnp.where(kblk == b, order[(b * NX + xh) * NZ + z], base)
    kpos = base * KR + kcol % KR
    first = NY * NX * NZ * KR - QW
    zrow = lax.broadcasted_iota(jnp.int32, (ZR, 1), 0)
    zpos = first + (((zrow // QR) % NY) * NX + zrow // (NY * QR)) * NZ * QR + zrow % QR

    for k in range(NX):
        for b in range(NY):
            slot = dn(xh, k, NX) * NY + b
            if k == 0:
                @pl.when(jnp.logical_not(own & (y == b)))
                def _():
                    arrived(p1.at[slot], r1.at[k, b])
            else:
                arrived(p1.at[slot], r1.at[k, b])
    zr, zl = up(z, 1, NZ), dn(z, 1, NZ)
    dzr, dzl = dev(s, y, xh, zr), dev(s, y, xh, zl)
    half = NB // 2

    def zref(d, t, h):
        src = dn(z, t, NZ) if d == 0 else up(z, t, NZ)
        return src, g.at[src, h]

    def zsend(d, t, h):
        _, ref = zref(d, t - 1, h)
        if t == NT:
            ref = ref.at[pl.ds(d * half, half)]
        go(rc(ref, ref, sz.at[d, t - 1, h], rz.at[d, t - 1, h], dzr if d == 0 else dzl))

    def zwait(d, t, h):
        _, ref = zref(d, t, h)
        if t == NT:
            ref = ref.at[pl.ds(d * half, half)]
        arrived(ref, rz.at[d, t - 1, h])

    def dsend(d, t):
        src, _ = zref(d, t - 1, 0)
        go(rc(gd.at[src], gd.at[src], szd.at[d, t - 1], rzd.at[d, t - 1], dzr if d == 0 else dzl))

    def dwait(d, t):
        src, _ = zref(d, t, 0)
        arrived(gd.at[src], rzd.at[d, t - 1])

    def delta_rows(zc):
        tile = gd[zc]
        for b in range(NB):
            piece = tile if b == 0 else pltpu.roll(tile, 128 - b * QR, 1)
            delc[pl.ds(pl.multiple_of(zc * ZR + b * QR, QR), QR)] = piece

    def chunks(t):
        return (z, up(z, NT, NZ)) if t == NT else (dn(z, t, NZ), up(z, t, NZ))

    def rowsof(zc):
        return pl.ds(pl.multiple_of(zc * ZR, ZR), ZR)

    def pair(ref, h, t):
        a, b = chunks(t)
        return jnp.concatenate([ref[h, rowsof(a)], ref[h, rowsof(b)]], axis=0)

    def put(ref, h, t, v):
        a, b = chunks(t)
        ref[h, rowsof(a)] = v[:ZR]
        ref[h, rowsof(b)] = v[ZR:]

    def score_tile(h, t):
        qs_ = []
        for zc in chunks(t):
            blk = g[zc, h].astype(F32).reshape(NB, 2, QR, HD)
            qc = blk[:, 0].reshape(ZR, HD).astype(BF16)
            q3[h, rowsof(zc)] = qc
            do3[h, rowsof(zc)] = blk[:, 1].reshape(ZR, HD).astype(BF16)
            qs_.append(qc)
        kh = kv[:, h, 0].reshape(KV, HD)
        sc = nt(jnp.concatenate(qs_, axis=0), kh) * SCALE
        a, b = chunks(t)
        qpos = jnp.concatenate([zpos + a * QR, zpos + b * QR], axis=0)
        sc = jnp.where(kpos <= qpos, sc, MASKED)
        m = jnp.max(sc, axis=1, keepdims=True)
        p = jnp.exp(sc - m)
        l = jnp.sum(p, axis=1, keepdims=True)
        put(pu, h, t, p)
        put(m3, h, t, jnp.broadcast_to(m, (RT, 128)))
        put(lse3, h, t, jnp.broadcast_to(m + jnp.log(l), (RT, 128)))

    def dprob_tile(h, t):
        vh = kv[:, h, 1].reshape(KV, HD)
        a, b = chunks(t)
        dl = jnp.concatenate([delc[rowsof(a)], delc[rowsof(b)]], axis=0)[:, h:h + 1]
        dp = nt(pair(do3, h, t), vh)
        put(ds0, h, t, pair(pu, h, t) * (dp - dl) * SCALE)

    lane2 = lax.broadcasted_iota(jnp.int32, (RT, 128), 1)

    def stats_send(gi):
        heads = GROUPS[gi]
        st = jnp.zeros((RT, 128), F32)
        for hi_, h in enumerate(heads):
            for rt in range(NR):
                st = jnp.where(lane2 == hi_ * NR + rt, lse3[h, rt * RT:(rt + 1) * RT], st)
        lz[gi, mz] = st.T[:16]
        for j in range(NZ):
            for k in range(NX):
                if (j, k) != (0, 0):
                    to = dev(s, y, up(xh, k, NX), up(z, j, NZ))
                    go(rc(lz.at[gi, mz], lz.at[gi, mz], sl.at[gi, k, j], rl.at[gi, k, j], to))

    mz = xh * NZ + z

    def stats_wait(gi):
        for j in range(NZ):
            for k in range(NX):
                if (j, k) != (0, 0):
                    f = dn(xh, k, NX) * NZ + dn(z, j, NZ)
                    arrived(lz.at[gi, f], rl.at[gi, k, j])
        mx = lz[gi, 0]
        for f in range(1, NX * NZ):
            mx = jnp.maximum(mx, lz[gi, f])
        tot = jnp.exp(lz[gi, 0] - mx)
        for f in range(1, NX * NZ):
            tot = tot + jnp.exp(lz[gi, f] - mx)
        lt = mx + jnp.log(tot)
        tt = jnp.concatenate([lt, jnp.zeros((112, 128), F32)], axis=0).T
        for hi_, h in enumerate(GROUPS[gi]):
            for rt in range(NR):
                rows = slice(rt * RT, (rt + 1) * RT)
                i = hi_ * NR + rt
                c3[h, rows] = jnp.exp(m3[h, rows] - jnp.broadcast_to(tt[:, i:i + 1], (RT, 128)))

    for h in range(HG):
        for b in range(NB):
            g[z, h, b] = p1[b, h]
    tile = jnp.zeros((QR, 128), F32)
    for b in range(NB):
        d2 = p1[b, HG].astype(F32)
        top = d2[:QR]
        d1 = jnp.where(lane < QR, top + d2[QR:] + pltpu.roll(top, 128 - QR, 1), 0.0)
        tile = tile + (d1 if b == 0 else pltpu.roll(d1, b * QR, 1))
    gd[z] = tile

    order_ = sorted((h + 3 * (t - 1), t, h) for t in range(1, NT + 2) for h in range(HG))
    late = []
    for _, t, h in order_:
        if t > 1:
            zwait(0, t - 1, h)
            zwait(1, t - 1, h)
        if t <= NT:
            zsend(0, t, h)
            zsend(1, t, h)
        if h == 0:
            if t > 1:
                dwait(0, t - 1)
                if t <= NT:
                    dwait(1, t - 1)
            if t <= NT:
                dsend(0, t)
                if t < NT:
                    dsend(1, t)
        if t == 1:
            kv_forward(h)
        if t > 1:
            if h == 0:
                for zc in chunks(t - 1):
                    delta_rows(zc)
            if t == 2:
                kv_ready(h)
            score_tile(h, t - 1)
            if t <= NT:
                dprob_tile(h, t - 1)
            else:
                late.append(h)
            if t == NT + 1:
                for gi, heads in enumerate(GROUPS):
                    if h == heads[-1]:
                        stats_send(gi)
                        for hh in late:
                            dprob_tile(hh, NT)
                        late = []

    def grads(h):
        kh = kv[:, h, 0].reshape(KV, HD)
        for rt in range(NR):
            rows = slice(rt * RT, (rt + 1) * RT)
            cc = c3[h, rows][:, :1]
            pbs[rows] = (pu[h, rows] * cc).astype(BF16)
            dbs[rows] = (ds0[h, rows] * cc).astype(BF16)
        dq = nn(dbs[...], kh)
        dqa[h] = dq.reshape(NZ, ZR, HD)
        qs[h] = dq.reshape(NZ, ZR, HD).astype(BF16)
        for j in range(1, NZ):
            t = up(z, j, NZ)
            go(rc(qs.at[h, t], qr.at[h, z], sg.at[h, j], rg.at[h, j], dev(s, y, xh, t)))
        dkt = tn(q3[h], dbs[...])
        dvt = tn(do3[h], pbs[...])
        for b in range(NY):
            dkv[h, b, 0] = dkt[:, b * KR:(b + 1) * KR].T
            dkv[h, b, 1] = dvt[:, b * KR:(b + 1) * KR].T
        ks1[h, 0, 0] = dkv[h, y2, 0].astype(BF16)
        ks1[h, 0, 1] = dkv[h, yr, 1].astype(BF16)
        ks1[h, 1, 0] = dkv[h, y2, 1].astype(BF16)
        ks1[h, 1, 1] = dkv[h, yl, 0].astype(BF16)
        go(rc(ks1.at[h, 0], kr1.at[h, 0], sk.at[0, 0, h], rk.at[0, 0, h], dyr))
        go(rc(ks1.at[h, 1], kr1.at[h, 1], sk.at[0, 1, h], rk.at[0, 1, h], dyl))

    def second_leg(h):
        arrived(kr1.at[h, 0], rk.at[0, 0, h])
        ks2[h, 0] = (dkv[h, yr, 0] + kr1[h, 0, 0].astype(F32)).astype(BF16)
        go(rc(ks2.at[h, 0], kr2.at[h, 0], sk.at[1, 0, h], rk.at[1, 0, h], dyr))
        arrived(kr1.at[h, 1], rk.at[0, 1, h])
        ks2[h, 1] = (dkv[h, yl, 1] + kr1[h, 1, 0].astype(F32)).astype(BF16)
        go(rc(ks2.at[h, 1], kr2.at[h, 1], sk.at[1, 1, h], rk.at[1, 1, h], dyl))

    def query_sum(h):
        acc = dqa[h, z]
        for j in range(1, NZ):
            f = dn(z, j, NZ)
            arrived(qr.at[h, f], rg.at[h, j])
            acc = acc + qr[h, f].astype(F32)
        tb[:, h] = acc.reshape(NB, QR, HD)

    def cache_out(h):
        arrived(kr2.at[h, 0], rk.at[1, 0, h])
        arrived(kr2.at[h, 1], rk.at[1, 1, h])
        cols = slice(h * HD, (h + 1) * HD)
        dk_out[:, cols] = (dkv[h, y, 0] + kr1[h, 1, 1].astype(F32) + kr2[h, 0].astype(F32)).astype(BF16)
        dv_out[:, cols] = (dkv[h, y, 1] + kr1[h, 0, 1].astype(F32) + kr2[h, 1].astype(F32)).astype(BF16)

    for gi, heads in enumerate(GROUPS):
        stats_wait(gi)
        for h in heads:
            grads(h)
            if h > 0:
                second_leg(h - 1)
                query_sum(h - 1)
    second_leg(HG - 1)
    query_sum(HG - 1)

    for j in range(NY):
        for k in range(NX):
            ty, tx = up(y, j, NY), up(xh, k, NX)
            cp = rc(tb.at[tx * NY + ty], p8.at[k, s], s8.at[j, k], r8.at[k, s], dev(y, ty, tx, z))
            if (j, k) == (0, 0):
                self_out = cp

                @pl.when(jnp.logical_not(own))
                def _():
                    cp.start()
            else:
                go(cp)

    @pl.when(own)
    def _():
        p8[0, s] = tb[mine]

    for h in range(HG):
        cache_out(h)

    for k in range(NX):
        for b in range(NS):
            if k == 0:
                @pl.when(jnp.logical_not(own & (s == b)))
                def _():
                    arrived(p8.at[k, b], r8.at[k, b])
            else:
                arrived(p8.at[k, b], r8.at[k, b])
    for b in range(NS):
        for h in range(HG):
            col = b * GF + h * HD
            dq_out[0, :, col:col + HD] = (p8[0, b, h] + p8[1, b, h]).astype(BF16)

    @pl.when(jnp.logical_not(own))
    def _():
        self_in.wait_send()
        self_out.wait_send()

    for cp in sends:
        cp.wait_send()


def local(block_order, queries, cache_keys, cache_values, attention_out, output_grad):
    dma = pltpu.SemaphoreType.DMA
    vm = pltpu.VMEM
    row = queries.shape
    scratch = [
        vm(row, BF16), vm(row, BF16), vm(row, BF16), vm((KR, GF), BF16), vm((KR, GF), BF16),
        vm((NS, HG + 1, 16, HD), BF16), vm((NB, HG + 1, 16, HD), BF16),
        vm((NZ, HG, NB, 16, HD), BF16), vm((NZ, QR, 128), F32),
        vm((NY, HG, 2, KR, HD), BF16), vm((HG, QW, HD), BF16), vm((HG, QW, HD), BF16), vm((QW, 128), F32),
        vm((HG, QW, KV), F32), vm((HG, QW, KV), F32),
        vm((HG, QW, 128), F32), vm((HG, QW, 128), F32), vm((HG, QW, 128), F32),
        vm((2, NX * NZ, 16, 128), F32),
        vm((QW, KV), BF16), vm((QW, KV), BF16),
        vm((HG, NZ, ZR, HD), F32), vm((HG, NZ, ZR, HD), BF16), vm((HG, NZ, ZR, HD), BF16),
        vm((HG, NY, 2, KR, HD), F32),
        vm((HG, 2, 2, KR, HD), BF16), vm((HG, 2, 2, KR, HD), BF16),
        vm((HG, 2, KR, HD), BF16), vm((HG, 2, KR, HD), BF16),
        vm((NB, HG, QR, HD), F32), vm((NX, NS, HG, QR, HD), F32),
        dma((5,)), dma((NS, NX)), dma((NX, NY)),
        dma((2, NT, HG)), dma((2, NT, HG)), dma((2, NT)), dma((2, NT)),
        dma((2, HG)), dma((2, HG)), dma((2, HG)), dma((2, HG)),
        dma((2, NX, NZ)), dma((2, NX, NZ)), dma((HG, NZ)), dma((HG, NZ)),
        dma((2, 2, HG)), dma((2, 2, HG)), dma((NY, NX)), dma((NX, NS)),
    ]
    vspec = pl.BlockSpec(memory_space=pltpu.VMEM)
    hbm = pl.BlockSpec(memory_space=pl.ANY)
    dq, dk, dv = pl.pallas_call(
        kernel,
        out_shape=(
            jax.ShapeDtypeStruct((1, QR, NS * GF), BF16),
            jax.ShapeDtypeStruct((KR, GF), BF16),
            jax.ShapeDtypeStruct((KR, GF), BF16),
        ),
        in_specs=[pl.BlockSpec(memory_space=pltpu.SMEM)] + [hbm] * 5,
        out_specs=(vspec, vspec, vspec),
        scratch_shapes=scratch,
        compiler_params=pltpu.CompilerParams(
            collective_id=0, has_side_effects=True, vmem_limit_bytes=56 << 20),
    )(block_order, queries, output_grad, attention_out, cache_keys, cache_values)
    return dq, dk, dv


def solution(mesh):
    in_specs = (
        P(),
        P("section", "ctx", None),
        P("ctx", "section"),
        P("ctx", "section"),
        P("section", "ctx", None),
        P("section", "ctx", None),
    )
    out_specs = (P("section", "ctx", None), P("ctx", "section"), P("ctx", "section"))
    return jax.shard_map(local, mesh=mesh, in_specs=in_specs, out_specs=out_specs, check_vma=False)
```

time: 1980 us -> 78.2 us (0.04); the launches traced: 1950 us -> 78.1 us
  blocking collectives: 1550 us -> 0 us
  matrix products: 134 us -> 0 us
  waiting for transfers between devices: 120 us -> 0 us
  loops' own time: 79 us -> 0 us
  Pallas kernels: 0 us -> 73.7 us
  local copies, waits for them, and re-layouts: 55.8 us -> 3.7 us
    unnamed x1 -> x0, blocking collectives: 777 us -> none
    pmax x1 -> x0, blocking collectives: 297 us -> none  [local(): lax.pmax(row_max.astype(jnp.bfloat16), 'ctx').astype(row_max.dtype)]
    psum x1 -> x0, blocking collectives: 297 us -> none  [local(): row_sum = lax.psum(row_sum * jnp.exp(row_max - peak_max), 'ctx')]
    all_gather x3 -> x0, blocking collectives: 175 us -> none  [the longest x1 157 us: local(): delta_all = lax.all_gather(delta_part, 'ctx', axis=1, tiled=True)]
    dot_general x120 -> x0, matrix products: 134 us -> none  [the longest x40 45.1 us: masked_scores(): jnp.dot(query_head, key_heads[head_index].T, preferred_element_type=jnp.f...]
    reduce_scatter x2 -> x0, waiting for transfers between devices: 118 us -> none  [the longest x1 61 us: local(): lax.psum_scatter(key_sum.astype(jnp.bfloat16), 'section', scatter_dimensi...]
    another operation x2 -> x0, loops' own time: 79 us -> none  [the longest x1 39.6 us: local(): row_max, row_sum = lax.map(local_stats, (query_heads, head_ids))]
    pallas_call x0 -> x1, Pallas kernels: none -> 73.7 us  [local(): pl.pallas_call(kernel, out_shape=(jax.ShapeDtypeStruct((1, QR, NS * GF),...]
  transfers between devices with their start and end apart: 4 -> 0, of which waited for: 2 -> 0; matrix products, arithmetic and copies ran while one was open for 3% -> 0% of each run, Pallas kernels for 0% -> 0%
where the time goes in v2:
time: 78.2 us; the launch traced here: 78.1 us
  Pallas kernels  73.7 us (94%)
  local copies, waits for them, and re-layouts  3.7 us (5%)
    pallas_call x1, Pallas kernels, local(): pl.pallas_call(kernel, out_shape=(jax.ShapeDtypeStruct((1, QR, NS * GF),...  73.7 us
    unnamed x5, local copies, waits for them, and re-layouts  3.7 us

profile of v2, /device:TPU:1, one launch (start us, length us, event | category | flops | bytes accessed | tf_op | source)
XLA Modules:
  0.0 78.1 jit_solution(15654813462005084857)
XLA Ops:
  0.6 73.7 %shard_map.85 = (bf16[1,8,2560]{2,1,0:T(8,128)(2,1)}, bf16[128,640]{1,0:T(8,128)(2,1)}, bf16[128,640]{1,0:T(8,128)(2,1)}) custom-call(s32[64]{0:T(128)} %order.1, bf16[1,8,2560]{2,1,0:T(8,128)(2,1)} %q_in.1, bf16[1,8,2560]{2,1,0:T(8,128)(2,1)} %do_in.1, bf16[1,8,2560]{2,1,0:T(8,128)(2,1)} %o_in.1, bf16[128,640]{1,0:T(8,128)(2,1)} %k_in.1, bf16[128,640]{1,0:T(8,128)(2,1)} %v_in.1), custom_call_target="tpu_custom_call" | custom-call | tf_op jit(solution)/shard_map/pallas_call | solution.py:472
  74.4 1.4 %copy.12 = bf16[1,8,2560]{2,1,0:T(8,128)(2,1)} copy(bf16[1,8,2560]{2,1,0:T(8,128)(2,1)} %get-tuple-element.6) | data formatting | bytes 81920
  75.8 0.0 copy-start
  75.8 1.6 %copy.13 = bf16[128,640]{1,0:T(8,128)(2,1)} copy(bf16[128,640]{1,0:T(8,128)(2,1)} %get-tuple-element.7) | data formatting | bytes 327680
  77.4 0.0 copy-done
  77.4 0.7 copy.14
Async XLA Ops:
  75.8 1.6 %copy-start = (bf16[128,640]{1,0:T(8,128)(2,1)S(1)}, bf16[128,640]{1,0:T(8,128)(2,1)}, u32[]{:S(2)}) copy-start(bf16[128,640]{1,0:T(8,128)(2,1)} %get-tuple-element.8) | copy-start | bytes 491524

commit v3 on v2

--- a/solution.py
+++ b/solution.py
@@ -38,19 +38,19 @@
 
 
 def kernel(order, q_in, do_in, o_in, k_in, v_in, dq_out, dk_out, dv_out,
-           qv, dov, ov, kin, vin, pk, p1, g, gd, kv, q3, do3, delc, pu, ds0, m3, lse3, c3, lz,
-           pbs, dbs, dqa, qs, qr, dkv, ks1, kr1, ks2, kr2, tb, p8,
+           qv, dov, ov, kin, vin, pk, p1, g, gd, kv, q3, do3, delc, pl_, pb, db, m3, lse3, c3, lz,
+           dqa, zs, zr_, dkv, ks1, kr1, ks2, kr2, tb, p8,
            sin, s1, r1, sz, rz, szd, rzd, sy, ry, sf, rf, sl, rl, sg, rg, sk, rk, s8, r8):
     s = lax.axis_index("section")
     c = lax.axis_index("ctx")
-    y = c // (NX * NZ)
-    xh = (c // NZ) % NX
-    z = c % NZ
+    y = c >> 4
+    xh = (c >> 3) & 1
+    z = c & 7
     me = (s, c)
     own = s == y
 
     def dev(s_, y_, x_, z_):
-        return (s_, (y_ * NX + x_) * NZ + z_)
+        return (s_, (y_ << 4) | (x_ << 3) | z_)
 
     def rc(src, dst, ssem, rsem, to):
         return pltpu.make_async_remote_copy(
@@ -61,16 +61,22 @@
         rc(dst, dst, rsem, rsem, me).wait_recv()
 
     def up(v, n, mod):
-        return (v + n) % mod
+        return (v + n) & (mod - 1)
 
     def dn(v, n, mod):
-        return (v + mod - n) % mod
+        return (v - n) & (mod - 1)
 
     sends = []
 
     def go(cp):
         cp.start()
         sends.append(cp)
+
+    loads = []
+    for i, (a, b) in enumerate(((q_in, qv), (do_in, dov), (o_in, ov), (k_in, kin), (v_in, vin))):
+        cp = pltpu.make_async_copy(a, b, sin.at[i])
+        cp.start()
+        loads.append(cp)
 
     yr, yl, y2 = up(y, 1, NY), dn(y, 1, NY), up(y, 2, NY)
     bar = pltpu.get_barrier_semaphore()
@@ -99,11 +105,6 @@
         greet(dev(s, s, xh, z))
         greet(dev(y, y, xh, z))
 
-    loads = []
-    for i, (a, b) in enumerate(((q_in, qv), (do_in, dov), (o_in, ov), (k_in, kin), (v_in, vin))):
-        cp = pltpu.make_async_copy(a, b, sin.at[i])
-        cp.start()
-        loads.append(cp)
     for cp in loads:
         cp.wait()
 
@@ -230,13 +231,15 @@
         ref[h, rowsof(b)] = v[ZR:]
 
     def score_tile(h, t):
-        qs_ = []
+        qs_, ds_ = [], []
         for zc in chunks(t):
             blk = g[zc, h].astype(F32).reshape(NB, 2, QR, HD)
             qc = blk[:, 0].reshape(ZR, HD).astype(BF16)
+            dc = blk[:, 1].reshape(ZR, HD).astype(BF16)
             q3[h, rowsof(zc)] = qc
-            do3[h, rowsof(zc)] = blk[:, 1].reshape(ZR, HD).astype(BF16)
+            do3[h, rowsof(zc)] = dc
             qs_.append(qc)
+            ds_.append(dc)
         kh = kv[:, h, 0].reshape(KV, HD)
         sc = nt(jnp.concatenate(qs_, axis=0), kh) * SCALE
         a, b = chunks(t)
@@ -245,16 +248,24 @@
         m = jnp.max(sc, axis=1, keepdims=True)
         p = jnp.exp(sc - m)
         l = jnp.sum(p, axis=1, keepdims=True)
-        put(pu, h, t, p)
+        put(pb, h, t, p.astype(BF16))
         put(m3, h, t, jnp.broadcast_to(m, (RT, 128)))
         put(lse3, h, t, jnp.broadcast_to(m + jnp.log(l), (RT, 128)))
-
-    def dprob_tile(h, t):
+        if t == NT:
+            pl_[h] = p
+        else:
+            dprob(h, t, p, jnp.concatenate(ds_, axis=0))
+
+    def dprob(h, t, p, dom):
         vh = kv[:, h, 1].reshape(KV, HD)
         a, b = chunks(t)
         dl = jnp.concatenate([delc[rowsof(a)], delc[rowsof(b)]], axis=0)[:, h:h + 1]
-        dp = nt(pair(do3, h, t), vh)
-        put(ds0, h, t, pair(pu, h, t) * (dp - dl) * SCALE)
+        put(db, h, t, (p * (nt(dom, vh) - dl) * SCALE).astype(BF16))
+
+    def dprob_late(h):
+        dprob(h, NT, pl_[h], pair(do3, h, NT))
+        kh = kv[:, h, 0].reshape(KV, HD)
+        dqa[h] = nn(db[h], kh).reshape(NZ, ZR, HD)
 
     lane2 = lax.broadcasted_iota(jnp.int32, (RT, 128), 1)
 
@@ -304,60 +315,99 @@
         tile = tile + (d1 if b == 0 else pltpu.roll(d1, b * QR, 1))
     gd[z] = tile
 
-    order_ = sorted((h + 3 * (t - 1), t, h) for t in range(1, NT + 2) for h in range(HG))
+    for h in range(HG):
+        zsend(0, 1, h)
+        zsend(1, 1, h)
+    dsend(0, 1)
+    dsend(1, 1)
+    kv_forward(0)
+    kv_forward(1)
     late = []
-    for _, t, h in order_:
-        if t > 1:
+    for t in range(2, NT + 2):
+        for h in range(HG):
             zwait(0, t - 1, h)
             zwait(1, t - 1, h)
-        if t <= NT:
-            zsend(0, t, h)
-            zsend(1, t, h)
-        if h == 0:
-            if t > 1:
+            if t <= NT:
+                zsend(0, t, h)
+                zsend(1, t, h)
+            if h == 0:
                 dwait(0, t - 1)
                 if t <= NT:
                     dwait(1, t - 1)
-            if t <= NT:
-                dsend(0, t)
-                if t < NT:
-                    dsend(1, t)
-        if t == 1:
-            kv_forward(h)
-        if t > 1:
-            if h == 0:
+                    dsend(0, t)
+                    if t < NT:
+                        dsend(1, t)
                 for zc in chunks(t - 1):
                     delta_rows(zc)
             if t == 2:
+                if h + 2 < HG:
+                    kv_forward(h + 2)
                 kv_ready(h)
             score_tile(h, t - 1)
-            if t <= NT:
-                dprob_tile(h, t - 1)
-            else:
+            if t == NT + 1:
                 late.append(h)
-            if t == NT + 1:
                 for gi, heads in enumerate(GROUPS):
                     if h == heads[-1]:
                         stats_send(gi)
                         for hh in late:
-                            dprob_tile(hh, NT)
+                            dprob_late(hh)
                         late = []
 
-    def grads(h):
-        kh = kv[:, h, 0].reshape(KV, HD)
-        for rt in range(NR):
-            rows = slice(rt * RT, (rt + 1) * RT)
-            cc = c3[h, rows][:, :1]
-            pbs[rows] = (pu[h, rows] * cc).astype(BF16)
-            dbs[rows] = (ds0[h, rows] * cc).astype(BF16)
-        dq = nn(dbs[...], kh)
-        dqa[h] = dq.reshape(NZ, ZR, HD)
-        qs[h] = dq.reshape(NZ, ZR, HD).astype(BF16)
-        for j in range(1, NZ):
-            t = up(z, j, NZ)
-            go(rc(qs.at[h, t], qr.at[h, z], sg.at[h, j], rg.at[h, j], dev(s, y, xh, t)))
-        dkt = tn(q3[h], dbs[...])
-        dvt = tn(do3[h], pbs[...])
+    HR = ZR // 2
+    dz2r, dz2l = dev(s, y, xh, up(z, 2, NZ)), dev(s, y, xh, dn(z, 2, NZ))
+
+    def zmsg(gi, d, kind):
+        heads = GROUPS[gi]
+        hs = pl.ds(heads[0], len(heads))
+        a_, b_ = zs.at[d, kind, hs], zr_.at[d, kind, hs]
+        if kind == 0:
+            part = pl.ds(d * HR, HR)
+            a_, b_ = zs.at[d, kind, hs, part], zr_.at[d, kind, hs, part]
+        near, far = (dzr, dz2r) if d == 0 else (dzl, dz2l)
+        return rc(a_, b_, sg.at[gi, d, kind], rg.at[gi, d, kind], far if kind in (0, 3) else near)
+
+    def step(d, n):
+        return up(z, n, NZ) if d == 0 else dn(z, n, NZ)
+
+    def query_grads(gi):
+        for h in GROUPS[gi]:
+            dqa[h] = dqa[h] * c3[h].reshape(NZ, ZR, HD)
+        for kind, n in ((0, 4), (1, 3), (2, 1)):
+            for d in range(2):
+                for h in GROUPS[gi]:
+                    if kind == 0:
+                        part = slice(d * HR, (d + 1) * HR)
+                        zs[d, kind, h, part] = dqa[h, step(d, n), part].astype(BF16)
+                    else:
+                        zs[d, kind, h] = dqa[h, step(d, n)].astype(BF16)
+                go(zmsg(gi, d, kind))
+
+    def query_relay(gi):
+        for d in range(2):
+            zmsg(gi, d, 0).wait_recv()
+            zmsg(gi, d, 1).wait_recv()
+            part = slice(d * HR, (d + 1) * HR)
+            rest = slice((1 - d) * HR, (2 - d) * HR)
+            for h in GROUPS[gi]:
+                acc = dqa[h, step(d, 2)] + zr_[d, 1, h].astype(F32)
+                zs[d, 3, h, rest] = acc[rest].astype(BF16)
+                zs[d, 3, h, part] = (acc[part] + zr_[d, 0, h, part].astype(F32)).astype(BF16)
+            go(zmsg(gi, d, 3))
+
+    def query_sum(gi):
+        for d in range(2):
+            zmsg(gi, d, 2).wait_recv()
+            zmsg(gi, d, 3).wait_recv()
+        for h in GROUPS[gi]:
+            acc = dqa[h, z]
+            for d in range(2):
+                acc = acc + zr_[d, 2, h].astype(F32) + zr_[d, 3, h].astype(F32)
+            tb[:, h] = acc.reshape(NB, QR, HD)
+
+    def cache_grads(h):
+        cc = c3[h]
+        dkt = tn((q3[h].astype(F32) * cc).astype(BF16), db[h])
+        dvt = tn((do3[h].astype(F32) * cc).astype(BF16), pb[h])
         for b in range(NY):
             dkv[h, b, 0] = dkt[:, b * KR:(b + 1) * KR].T
             dkv[h, b, 1] = dvt[:, b * KR:(b + 1) * KR].T
@@ -376,14 +426,6 @@
         ks2[h, 1] = (dkv[h, yl, 1] + kr1[h, 1, 0].astype(F32)).astype(BF16)
         go(rc(ks2.at[h, 1], kr2.at[h, 1], sk.at[1, 1, h], rk.at[1, 1, h], dyl))
 
-    def query_sum(h):
-        acc = dqa[h, z]
-        for j in range(1, NZ):
-            f = dn(z, j, NZ)
-            arrived(qr.at[h, f], rg.at[h, j])
-            acc = acc + qr[h, f].astype(F32)
-        tb[:, h] = acc.reshape(NB, QR, HD)
-
     def cache_out(h):
         arrived(kr2.at[h, 0], rk.at[1, 0, h])
         arrived(kr2.at[h, 1], rk.at[1, 1, h])
@@ -391,15 +433,24 @@
         dk_out[:, cols] = (dkv[h, y, 0] + kr1[h, 1, 1].astype(F32) + kr2[h, 0].astype(F32)).astype(BF16)
         dv_out[:, cols] = (dkv[h, y, 1] + kr1[h, 0, 1].astype(F32) + kr2[h, 1].astype(F32)).astype(BF16)
 
-    for gi, heads in enumerate(GROUPS):
-        stats_wait(gi)
-        for h in heads:
-            grads(h)
-            if h > 0:
-                second_leg(h - 1)
-                query_sum(h - 1)
-    second_leg(HG - 1)
-    query_sum(HG - 1)
+    stats_wait(0)
+    query_grads(0)
+    cache_grads(0)
+    cache_grads(1)
+    cache_grads(2)
+    second_leg(0)
+    query_relay(0)
+    stats_wait(1)
+    query_grads(1)
+    second_leg(1)
+    cache_grads(3)
+    second_leg(2)
+    cache_grads(4)
+    query_sum(0)
+    query_relay(1)
+    second_leg(3)
+    second_leg(4)
+    query_sum(1)
 
     for j in range(NY):
         for k in range(NX):
@@ -443,6 +494,12 @@
         cp.wait_send()
 
 
+def place(a, b, c, x, y, z):
+    x[...] = a[...]
+    y[...] = b[...]
+    z[...] = c[...]
+
+
 def local(block_order, queries, cache_keys, cache_values, attention_out, output_grad):
     dma = pltpu.SemaphoreType.DMA
     vm = pltpu.VMEM
@@ -452,11 +509,10 @@
         vm((NS, HG + 1, 16, HD), BF16), vm((NB, HG + 1, 16, HD), BF16),
         vm((NZ, HG, NB, 16, HD), BF16), vm((NZ, QR, 128), F32),
         vm((NY, HG, 2, KR, HD), BF16), vm((HG, QW, HD), BF16), vm((HG, QW, HD), BF16), vm((QW, 128), F32),
-        vm((HG, QW, KV), F32), vm((HG, QW, KV), F32),
+        vm((HG, RT, KV), F32), vm((HG, QW, KV), BF16), vm((HG, QW, KV), BF16),
         vm((HG, QW, 128), F32), vm((HG, QW, 128), F32), vm((HG, QW, 128), F32),
         vm((2, NX * NZ, 16, 128), F32),
-        vm((QW, KV), BF16), vm((QW, KV), BF16),
-        vm((HG, NZ, ZR, HD), F32), vm((HG, NZ, ZR, HD), BF16), vm((HG, NZ, ZR, HD), BF16),
+        vm((HG, NZ, ZR, HD), F32), vm((2, 4, HG, ZR, HD), BF16), vm((2, 4, HG, ZR, HD), BF16),
         vm((HG, NY, 2, KR, HD), F32),
         vm((HG, 2, 2, KR, HD), BF16), vm((HG, 2, 2, KR, HD), BF16),
         vm((HG, 2, KR, HD), BF16), vm((HG, 2, KR, HD), BF16),
@@ -464,7 +520,7 @@
         dma((5,)), dma((NS, NX)), dma((NX, NY)),
         dma((2, NT, HG)), dma((2, NT, HG)), dma((2, NT)), dma((2, NT)),
         dma((2, HG)), dma((2, HG)), dma((2, HG)), dma((2, HG)),
-        dma((2, NX, NZ)), dma((2, NX, NZ)), dma((HG, NZ)), dma((HG, NZ)),
+        dma((2, NX, NZ)), dma((2, NX, NZ)), dma((2, 2, 4)), dma((2, 2, 4)),
         dma((2, 2, HG)), dma((2, 2, HG)), dma((NY, NX)), dma((NX, NS)),
     ]
     vspec = pl.BlockSpec(memory_space=pltpu.VMEM)
@@ -482,7 +538,12 @@
         compiler_params=pltpu.CompilerParams(
             collective_id=0, has_side_effects=True, vmem_limit_bytes=56 << 20),
     )(block_order, queries, output_grad, attention_out, cache_keys, cache_values)
-    return dq, dk, dv
+    return pl.pallas_call(
+        place,
+        out_shape=tuple(jax.ShapeDtypeStruct(v.shape, v.dtype) for v in (dq, dk, dv)),
+        in_specs=[vspec] * 3,
+        out_specs=(vspec,) * 3,
+    )(dq, dk, dv)
 
 
 def solution(mesh):

time: 78.2 us -> 70.9 us (0.907)
  local copies, waits for them, and re-layouts: 3.7 us -> 0 us
  Pallas kernels: 73.7 us -> 70.1 us
    pallas_call x1, Pallas kernels: 73.7 us -> 68.3 us  [local(): pl.pallas_call(kernel, out_shape=(jax.ShapeDtypeStruct((1, QR, NS * GF),...]
    unnamed x5 -> x0, local copies, waits for them, and re-layouts: 3.7 us -> none
    pallas_call x0 -> x1, Pallas kernels: none -> 1.76 us  [local(): pl.pallas_call(place, out_shape=tuple((jax.ShapeDtypeStruct(v.shape, v.dt...]
where the time goes in v3:
time: 70.9 us; the launch traced here: 70.8 us
  Pallas kernels  70.1 us (99%)
    pallas_call x1, Pallas kernels, local(): pl.pallas_call(kernel, out_shape=(jax.ShapeDtypeStruct((1, QR, NS * GF),...  68.3 us
    pallas_call x1, Pallas kernels, local(): pl.pallas_call(place, out_shape=tuple((jax.ShapeDtypeStruct(v.shape, v.dt...  1.76 us

profile of v3, /device:TPU:1, one launch (start us, length us, event | category | flops | bytes accessed | tf_op | source)
XLA Modules:
  0.0 70.8 jit_solution(1244182784349437026)
XLA Ops:
  0.6 68.3 %shard_map.85 = (bf16[1,8,2560]{2,1,0:T(8,128)(2,1)}, bf16[128,640]{1,0:T(8,128)(2,1)}, bf16[128,640]{1,0:T(8,128)(2,1)}) custom-call(s32[64]{0:T(128)} %order.1, bf16[1,8,2560]{2,1,0:T(8,128)(2,1)} %q_in.1, bf16[1,8,2560]{2,1,0:T(8,128)(2,1)} %do_in.1, bf16[1,8,2560]{2,1,0:T(8,128)(2,1)} %o_in.1, bf16[128,640]{1,0:T(8,128)(2,1)} %k_in.1, bf16[128,640]{1,0:T(8,128)(2,1)} %v_in.1), custom_call_target="tpu_custom_call" | custom-call | tf_op jit(solution)/shard_map/pallas_call | solution.py:528
  69.0 1.8 %shard_map.86 = (bf16[1,8,2560]{2,1,0:T(8,128)(2,1)}, bf16[128,640]{1,0:T(8,128)(2,1)}, bf16[128,640]{1,0:T(8,128)(2,1)}) custom-call(bf16[1,8,2560]{2,1,0:T(8,128)(2,1)} %get-tuple-element.6.a, bf16[128,640]{1,0:T(8,128)(2,1)} %get-tuple-element.7.b, bf16[128,640]{1,0:T(8,128)(2,1)} %get-tuple-element.8.c), custom_call_target="tpu_custom_call" | custom-call | tf_op jit(solution)/shard_map/pallas_call | solution.py:541

commit v4 on v3

--- a/solution.py
+++ b/solution.py
@@ -22,7 +22,8 @@
 MASKED = -1e30
 RT = 128
 NR = QW // RT
-GROUPS = ((0, 1, 2), (3, 4))
+PIECES = ((0, 2), (2, 3))
+SR = 24
 
 
 def nt(a, b):
@@ -38,7 +39,7 @@
 
 
 def kernel(order, q_in, do_in, o_in, k_in, v_in, dq_out, dk_out, dv_out,
-           qv, dov, ov, kin, vin, pk, p1, g, gd, kv, q3, do3, delc, pl_, pb, db, m3, lse3, c3, lz,
+           qv, dov, ov, kin, vin, pk, p1, g, gd, kv, q3, do3, delc, pl_, pb, db, m3, lse3, c3, w3, lz, wt,
            dqa, zs, zr_, dkv, ks1, kr1, ks2, kr2, tb, p8,
            sin, s1, r1, sz, rz, szd, rzd, sy, ry, sf, rf, sl, rl, sg, rg, sk, rk, s8, r8):
     s = lax.axis_index("section")
@@ -149,18 +150,23 @@
     for h in range(HG):
         kv[y, h, 0] = kin[:, h * HD:(h + 1) * HD]
         kv[y, h, 1] = vin[:, h * HD:(h + 1) * HD]
-        go(rc(kv.at[y, h], kv.at[y, h], sy.at[0, h], ry.at[0, h], dyr))
-        go(rc(kv.at[y, h], kv.at[y, h], sy.at[1, h], ry.at[1, h], dyl))
-
-    def kv_forward(h):
-        arrived(kv.at[yl, h], ry.at[0, h])
-        go(rc(kv.at[yl, h, 0], kv.at[yl, h, 0], sf.at[0, h], rf.at[0, h], dyr))
-        arrived(kv.at[yr, h], ry.at[1, h])
-        go(rc(kv.at[yr, h, 1], kv.at[yr, h, 1], sf.at[1, h], rf.at[1, h], dyl))
-
-    def kv_ready(h):
-        arrived(kv.at[y2, h, 0], rf.at[0, h])
-        arrived(kv.at[y2, h, 1], rf.at[1, h])
+        for i, (h0, n) in enumerate(PIECES):
+            if h == h0 + n - 1:
+                ref = kv.at[y, pl.ds(h0, n)]
+                go(rc(ref, ref, sy.at[0, i], ry.at[0, i], dyr))
+                go(rc(ref, ref, sy.at[1, i], ry.at[1, i], dyl))
+
+    def kv_forward(i):
+        hs = pl.ds(*PIECES[i])
+        arrived(kv.at[yl, hs], ry.at[0, i])
+        go(rc(kv.at[yl, hs, 0], kv.at[yl, hs, 0], sf.at[0, i], rf.at[0, i], dyr))
+        arrived(kv.at[yr, hs], ry.at[1, i])
+        go(rc(kv.at[yr, hs, 1], kv.at[yr, hs, 1], sf.at[1, i], rf.at[1, i], dyl))
+
+    def kv_ready(i):
+        hs = pl.ds(*PIECES[i])
+        arrived(kv.at[y2, hs, 0], rf.at[0, i])
+        arrived(kv.at[y2, hs, 1], rf.at[1, i])
 
     kcol = lax.broadcasted_iota(jnp.int32, (1, KV), 1)
     kblk = kcol // KR
@@ -185,28 +191,24 @@
     dzr, dzl = dev(s, y, xh, zr), dev(s, y, xh, zl)
     half = NB // 2
 
-    def zref(d, t, h):
+    def zref(d, t, i, part):
         src = dn(z, t, NZ) if d == 0 else up(z, t, NZ)
-        return src, g.at[src, h]
-
-    def zsend(d, t, h):
-        _, ref = zref(d, t - 1, h)
-        if t == NT:
-            ref = ref.at[pl.ds(d * half, half)]
-        go(rc(ref, ref, sz.at[d, t - 1, h], rz.at[d, t - 1, h], dzr if d == 0 else dzl))
-
-    def zwait(d, t, h):
-        _, ref = zref(d, t, h)
-        if t == NT:
-            ref = ref.at[pl.ds(d * half, half)]
-        arrived(ref, rz.at[d, t - 1, h])
+        hs = pl.ds(*PIECES[i])
+        return g.at[src, hs, pl.ds(d * half, half)] if part else g.at[src, hs]
+
+    def zsend(d, t, i):
+        ref = zref(d, t - 1, i, t == NT)
+        go(rc(ref, ref, sz.at[d, t - 1, i], rz.at[d, t - 1, i], dzr if d == 0 else dzl))
+
+    def zwait(d, t, i):
+        arrived(zref(d, t, i, t == NT), rz.at[d, t - 1, i])
 
     def dsend(d, t):
-        src, _ = zref(d, t - 1, 0)
+        src = dn(z, t - 1, NZ) if d == 0 else up(z, t - 1, NZ)
         go(rc(gd.at[src], gd.at[src], szd.at[d, t - 1], rzd.at[d, t - 1], dzr if d == 0 else dzl))
 
     def dwait(d, t):
-        src, _ = zref(d, t, 0)
+        src = dn(z, t, NZ) if d == 0 else up(z, t, NZ)
         arrived(gd.at[src], rzd.at[d, t - 1])
 
     def delta_rows(zc):
@@ -265,44 +267,60 @@
     def dprob_late(h):
         dprob(h, NT, pl_[h], pair(do3, h, NT))
         kh = kv[:, h, 0].reshape(KV, HD)
-        dqa[h] = nn(db[h], kh).reshape(NZ, ZR, HD)
+        dqa[h] = (nn(db[h], kh) * jnp.exp(m3[h] - lse3[h])).reshape(NZ, ZR, HD)
 
     lane2 = lax.broadcasted_iota(jnp.int32, (RT, 128), 1)
 
-    def stats_send(gi):
-        heads = GROUPS[gi]
+    mz = xh * NZ + z
+
+    def stats_send():
         st = jnp.zeros((RT, 128), F32)
-        for hi_, h in enumerate(heads):
+        for h in range(HG):
             for rt in range(NR):
-                st = jnp.where(lane2 == hi_ * NR + rt, lse3[h, rt * RT:(rt + 1) * RT], st)
-        lz[gi, mz] = st.T[:16]
+                st = jnp.where(lane2 == h * NR + rt, lse3[h, rt * RT:(rt + 1) * RT], st)
+        lz[mz] = st.T[:SR]
         for j in range(NZ):
             for k in range(NX):
                 if (j, k) != (0, 0):
                     to = dev(s, y, up(xh, k, NX), up(z, j, NZ))
-                    go(rc(lz.at[gi, mz], lz.at[gi, mz], sl.at[gi, k, j], rl.at[gi, k, j], to))
-
-    mz = xh * NZ + z
-
-    def stats_wait(gi):
+                    go(rc(lz.at[mz], lz.at[mz], sl.at[k, j], rl.at[k, j], to))
+
+    def stats_wait():
         for j in range(NZ):
             for k in range(NX):
                 if (j, k) != (0, 0):
-                    f = dn(xh, k, NX) * NZ + dn(z, j, NZ)
-                    arrived(lz.at[gi, f], rl.at[gi, k, j])
-        mx = lz[gi, 0]
+                    f = (up(xh, k, NX) << 3) | dn(z, j, NZ)
+                    arrived(lz.at[f], rl.at[k, j])
+        mx = lz[0]
         for f in range(1, NX * NZ):
-            mx = jnp.maximum(mx, lz[gi, f])
-        tot = jnp.exp(lz[gi, 0] - mx)
+            mx = jnp.maximum(mx, lz[f])
+        tot = jnp.exp(lz[0] - mx)
         for f in range(1, NX * NZ):
-            tot = tot + jnp.exp(lz[gi, f] - mx)
+            tot = tot + jnp.exp(lz[f] - mx)
         lt = mx + jnp.log(tot)
-        tt = jnp.concatenate([lt, jnp.zeros((112, 128), F32)], axis=0).T
-        for hi_, h in enumerate(GROUPS[gi]):
+        pad = jnp.zeros((128 - SR, 128), F32)
+        tt = jnp.concatenate([lt, pad], axis=0).T
+        for h in range(HG):
             for rt in range(NR):
                 rows = slice(rt * RT, (rt + 1) * RT)
-                i = hi_ * NR + rt
-                c3[h, rows] = jnp.exp(m3[h, rows] - jnp.broadcast_to(tt[:, i:i + 1], (RT, 128)))
+                i = h * NR + rt
+                col = jnp.broadcast_to(tt[:, i:i + 1], (RT, 128))
+                c3[h, rows] = jnp.exp(m3[h, rows] - col)
+                w3[h, rows] = jnp.exp(lse3[h, rows] - col)
+        return lt, pad
+
+    def weights(lt, pad):
+        for i, n in enumerate((-2, -1, 1, 2)):
+            f = (xh << 3) | up(z, n, NZ)
+            wt[i] = jnp.concatenate([jnp.exp(lz[f] - lt), pad], axis=0).T
+
+    lane3 = lax.broadcasted_iota(jnp.int32, (ZR, 128), 1)
+
+    def weight(n, zc, h):
+        i = {-2: 0, -1: 1, 1: 2, 2: 3}[n]
+        v = wt[i, pl.ds(pl.multiple_of((zc & 1) * ZR, ZR), ZR)]
+        v = jnp.where(lane3 == h * NR + (zc >> 1), v, 0.0)
+        return jnp.sum(v, axis=1, keepdims=True)
 
     for h in range(HG):
         for b in range(NB):
@@ -315,22 +333,21 @@
         tile = tile + (d1 if b == 0 else pltpu.roll(d1, b * QR, 1))
     gd[z] = tile
 
-    for h in range(HG):
-        zsend(0, 1, h)
-        zsend(1, 1, h)
-    dsend(0, 1)
-    dsend(1, 1)
+    for i in range(2):
+        zsend(0, 1, i)
+        zsend(1, 1, i)
+        if i == 0:
+            dsend(0, 1)
+            dsend(1, 1)
     kv_forward(0)
-    kv_forward(1)
-    late = []
     for t in range(2, NT + 2):
-        for h in range(HG):
-            zwait(0, t - 1, h)
-            zwait(1, t - 1, h)
+        for i, (h0, n) in enumerate(PIECES):
+            zwait(0, t - 1, i)
+            zwait(1, t - 1, i)
             if t <= NT:
-                zsend(0, t, h)
-                zsend(1, t, h)
-            if h == 0:
+                zsend(0, t, i)
+                zsend(1, t, i)
+            if i == 0:
                 dwait(0, t - 1)
                 if t <= NT:
                     dwait(1, t - 1)
@@ -340,68 +357,62 @@
                 for zc in chunks(t - 1):
                     delta_rows(zc)
             if t == 2:
-                if h + 2 < HG:
-                    kv_forward(h + 2)
-                kv_ready(h)
-            score_tile(h, t - 1)
-            if t == NT + 1:
-                late.append(h)
-                for gi, heads in enumerate(GROUPS):
-                    if h == heads[-1]:
-                        stats_send(gi)
-                        for hh in late:
-                            dprob_late(hh)
-                        late = []
+                if i == 0:
+                    kv_forward(1)
+                kv_ready(i)
+            for h in range(h0, h0 + n):
+                score_tile(h, t - 1)
+    stats_send()
 
     HR = ZR // 2
     dz2r, dz2l = dev(s, y, xh, up(z, 2, NZ)), dev(s, y, xh, dn(z, 2, NZ))
 
-    def zmsg(gi, d, kind):
-        heads = GROUPS[gi]
-        hs = pl.ds(heads[0], len(heads))
-        a_, b_ = zs.at[d, kind, hs], zr_.at[d, kind, hs]
+    def zmsg(d, kind):
+        a_, b_ = zs.at[d, kind], zr_.at[d, kind]
         if kind == 0:
             part = pl.ds(d * HR, HR)
-            a_, b_ = zs.at[d, kind, hs, part], zr_.at[d, kind, hs, part]
+            a_, b_ = zs.at[d, kind, :, part], zr_.at[d, kind, :, part]
         near, far = (dzr, dz2r) if d == 0 else (dzl, dz2l)
-        return rc(a_, b_, sg.at[gi, d, kind], rg.at[gi, d, kind], far if kind in (0, 3) else near)
+        return rc(a_, b_, sg.at[d, kind], rg.at[d, kind], far if kind in (0, 3) else near)
 
     def step(d, n):
         return up(z, n, NZ) if d == 0 else dn(z, n, NZ)
 
-    def query_grads(gi):
-        for h in GROUPS[gi]:
-            dqa[h] = dqa[h] * c3[h].reshape(NZ, ZR, HD)
-        for kind, n in ((0, 4), (1, 3), (2, 1)):
+    def query_grads():
+        for kind, n in ((1, 3), (0, 4), (2, 1)):
             for d in range(2):
-                for h in GROUPS[gi]:
+                for h in range(HG):
                     if kind == 0:
                         part = slice(d * HR, (d + 1) * HR)
                         zs[d, kind, h, part] = dqa[h, step(d, n), part].astype(BF16)
                     else:
                         zs[d, kind, h] = dqa[h, step(d, n)].astype(BF16)
-                go(zmsg(gi, d, kind))
-
-    def query_relay(gi):
+                go(zmsg(d, kind))
+
+    def query_relay():
         for d in range(2):
-            zmsg(gi, d, 0).wait_recv()
-            zmsg(gi, d, 1).wait_recv()
+            sign = 1 - 2 * d
+            zmsg(d, 0).wait_recv()
+            zmsg(d, 1).wait_recv()
             part = slice(d * HR, (d + 1) * HR)
             rest = slice((1 - d) * HR, (2 - d) * HR)
-            for h in GROUPS[gi]:
-                acc = dqa[h, step(d, 2)] + zr_[d, 1, h].astype(F32)
+            to = step(d, 2)
+            for h in range(HG):
+                acc = dqa[h, to] * w3[h, rowsof(to)] + zr_[d, 1, h].astype(F32) * weight(-sign, to, h)
+                far = zr_[d, 0, h, part].astype(F32) * weight(-2 * sign, to, h)[part]
                 zs[d, 3, h, rest] = acc[rest].astype(BF16)
-                zs[d, 3, h, part] = (acc[part] + zr_[d, 0, h, part].astype(F32)).astype(BF16)
-            go(zmsg(gi, d, 3))
-
-    def query_sum(gi):
+                zs[d, 3, h, part] = (acc[part] + far).astype(BF16)
+            go(zmsg(d, 3))
+
+    def query_sum():
         for d in range(2):
-            zmsg(gi, d, 2).wait_recv()
-            zmsg(gi, d, 3).wait_recv()
-        for h in GROUPS[gi]:
-            acc = dqa[h, z]
+            zmsg(d, 2).wait_recv()
+            zmsg(d, 3).wait_recv()
+        for h in range(HG):
+            acc = dqa[h, z] * w3[h, rowsof(z)]
             for d in range(2):
-                acc = acc + zr_[d, 2, h].astype(F32) + zr_[d, 3, h].astype(F32)
+                acc = acc + zr_[d, 3, h].astype(F32)
+                acc = acc + zr_[d, 2, h].astype(F32) * weight(2 * d - 1, z, h)
             tb[:, h] = acc.reshape(NB, QR, HD)
 
     def cache_grads(h):
@@ -433,24 +444,22 @@
         dk_out[:, cols] = (dkv[h, y, 0] + kr1[h, 1, 1].astype(F32) + kr2[h, 0].astype(F32)).astype(BF16)
         dv_out[:, cols] = (dkv[h, y, 1] + kr1[h, 0, 1].astype(F32) + kr2[h, 1].astype(F32)).astype(BF16)
 
-    stats_wait(0)
-    query_grads(0)
+    for h in range(HG):
+        dprob_late(h)
+    query_grads()
+    stats = stats_wait()
     cache_grads(0)
     cache_grads(1)
+    weights(*stats)
+    query_relay()
+    second_leg(0)
     cache_grads(2)
-    second_leg(0)
-    query_relay(0)
-    stats_wait(1)
-    query_grads(1)
     second_leg(1)
     cache_grads(3)
     second_leg(2)
     cache_grads(4)
-    query_sum(0)
-    query_relay(1)
     second_leg(3)
-    second_leg(4)
-    query_sum(1)
+    query_sum()
 
     for j in range(NY):
         for k in range(NX):
@@ -469,6 +478,7 @@
     def _():
         p8[0, s] = tb[mine]
 
+    second_leg(HG - 1)
     for h in range(HG):
         cache_out(h)
 
@@ -511,16 +521,16 @@
         vm((NY, HG, 2, KR, HD), BF16), vm((HG, QW, HD), BF16), vm((HG, QW, HD), BF16), vm((QW, 128), F32),
         vm((HG, RT, KV), F32), vm((HG, QW, KV), BF16), vm((HG, QW, KV), BF16),
         vm((HG, QW, 128), F32), vm((HG, QW, 128), F32), vm((HG, QW, 128), F32),
-        vm((2, NX * NZ, 16, 128), F32),
+        vm((HG, QW, 128), F32), vm((NX * NZ, SR, 128), F32), vm((4, 128, 128), F32),
         vm((HG, NZ, ZR, HD), F32), vm((2, 4, HG, ZR, HD), BF16), vm((2, 4, HG, ZR, HD), BF16),
         vm((HG, NY, 2, KR, HD), F32),
         vm((HG, 2, 2, KR, HD), BF16), vm((HG, 2, 2, KR, HD), BF16),
         vm((HG, 2, KR, HD), BF16), vm((HG, 2, KR, HD), BF16),
         vm((NB, HG, QR, HD), F32), vm((NX, NS, HG, QR, HD), F32),
         dma((5,)), dma((NS, NX)), dma((NX, NY)),
-        dma((2, NT, HG)), dma((2, NT, HG)), dma((2, NT)), dma((2, NT)),
-        dma((2, HG)), dma((2, HG)), dma((2, HG)), dma((2, HG)),
-        dma((2, NX, NZ)), dma((2, NX, NZ)), dma((2, 2, 4)), dma((2, 2, 4)),
+        dma((2, NT, 2)), dma((2, NT, 2)), dma((2, NT)), dma((2, NT)),
+        dma((2, 2)), dma((2, 2)), dma((2, 2)), dma((2, 2)),
+        dma((NX, NZ)), dma((NX, NZ)), dma((2, 4)), dma((2, 4)),
         dma((2, 2, HG)), dma((2, 2, HG)), dma((NY, NX)), dma((NX, NS)),
     ]
     vspec = pl.BlockSpec(memory_space=pltpu.VMEM)

time: 70.9 us -> 70.8 us (level); the launches traced: 70.8 us -> 69.6 us
  Pallas kernels: 70.1 us -> 68.9 us
    pallas_call x1, Pallas kernels: 68.3 us -> 67.2 us  [local(): pl.pallas_call(kernel, out_shape=(jax.ShapeDtypeStruct((1, QR, NS * GF),...]
where the time goes in v4:
time: 70.8 us; the launch traced here: 69.6 us
  Pallas kernels  68.9 us (97%)
    pallas_call x1, Pallas kernels, local(): pl.pallas_call(kernel, out_shape=(jax.ShapeDtypeStruct((1, QR, NS * GF),...  67.2 us
    pallas_call x1, Pallas kernels, local(): pl.pallas_call(place, out_shape=tuple((jax.ShapeDtypeStruct(v.shape, v.dt...  1.76 us

profile of v4, /device:TPU:1, one launch (start us, length us, event | category | flops | bytes accessed | tf_op | source)
XLA Modules:
  0.0 69.6 jit_solution(6339928686064032086)
XLA Ops:
  0.6 67.2 %shard_map.85 = (bf16[1,8,2560]{2,1,0:T(8,128)(2,1)}, bf16[128,640]{1,0:T(8,128)(2,1)}, bf16[128,640]{1,0:T(8,128)(2,1)}) custom-call(s32[64]{0:T(128)} %order.1, bf16[1,8,2560]{2,1,0:T(8,128)(2,1)} %q_in.1, bf16[1,8,2560]{2,1,0:T(8,128)(2,1)} %do_in.1, bf16[1,8,2560]{2,1,0:T(8,128)(2,1)} %o_in.1, bf16[128,640]{1,0:T(8,128)(2,1)} %k_in.1, bf16[128,640]{1,0:T(8,128)(2,1)} %v_in.1), custom_call_target="tpu_custom_call" | custom-call | tf_op jit(solution)/shard_map/pallas_call | solution.py:538
  67.8 1.8 %shard_map.86 = (bf16[1,8,2560]{2,1,0:T(8,128)(2,1)}, bf16[128,640]{1,0:T(8,128)(2,1)}, bf16[128,640]{1,0:T(8,128)(2,1)}) custom-call(bf16[1,8,2560]{2,1,0:T(8,128)(2,1)} %get-tuple-element.6.a, bf16[128,640]{1,0:T(8,128)(2,1)} %get-tuple-element.7.b, bf16[128,640]{1,0:T(8,128)(2,1)} %get-tuple-element.8.c), custom_call_target="tpu_custom_call" | custom-call | tf_op jit(solution)/shard_map/pallas_call | solution.py:551

commit v5 on v4

--- a/solution.py
+++ b/solution.py
@@ -39,9 +39,9 @@
 
 
 def kernel(order, q_in, do_in, o_in, k_in, v_in, dq_out, dk_out, dv_out,
-           qv, dov, ov, kin, vin, pk, p1, g, gd, kv, q3, do3, delc, pl_, pb, db, m3, lse3, c3, w3, lz, wt,
+           qv, dov, ov, kin, vin, pk, p1, g, gd, kv, q3, do3, delc, pl_, pb, db, m3, lse3, c3, w3, lx, lz, wt,
            dqa, zs, zr_, dkv, ks1, kr1, ks2, kr2, tb, p8,
-           sin, s1, r1, sz, rz, szd, rzd, sy, ry, sf, rf, sl, rl, sg, rg, sk, rk, s8, r8):
+           sin, s1, r1, sz, rz, szd, rzd, sy, ry, sf, rf, sl, rl, sx, rx, sg, rg, sk, rk, s8, r8):
     s = lax.axis_index("section")
     c = lax.axis_index("ctx")
     y = c >> 4
@@ -86,13 +86,11 @@
         pl.semaphore_signal(bar, inc=1, device_id=to, device_id_type=MESH)
 
     count = 0
-    for j in range(NZ):
-        for k in range(NX):
-            if (j, k) != (0, 0):
-                greet(dev(s, y, up(xh, k, NX), up(z, j, NZ)))
-                count += 1
-    for t in (yr, yl):
-        greet(dev(s, t, xh, z))
+    for j in range(1, NZ):
+        greet(dev(s, y, xh, up(z, j, NZ)))
+        count += 1
+    for t in (dev(s, yr, xh, z), dev(s, yl, xh, z), dev(s, y, up(xh, 1, NX), z)):
+        greet(t)
         count += 1
     for i in range(4):
         for k in range(NX):
@@ -189,6 +187,7 @@
                 arrived(p1.at[slot], r1.at[k, b])
     zr, zl = up(z, 1, NZ), dn(z, 1, NZ)
     dzr, dzl = dev(s, y, xh, zr), dev(s, y, xh, zl)
+    dz2r, dz2l = dev(s, y, xh, up(z, 2, NZ)), dev(s, y, xh, dn(z, 2, NZ))
     half = NB // 2
 
     def zref(d, t, i, part):
@@ -197,19 +196,22 @@
         return g.at[src, hs, pl.ds(d * half, half)] if part else g.at[src, hs]
 
     def zsend(d, t, i):
-        ref = zref(d, t - 1, i, t == NT)
-        go(rc(ref, ref, sz.at[d, t - 1, i], rz.at[d, t - 1, i], dzr if d == 0 else dzl))
+        last = t == NT
+        ref = zref(d, 2 if last else t - 1, i, last)
+        to = (dz2r if d == 0 else dz2l) if last else (dzr if d == 0 else dzl)
+        go(rc(ref, ref, sz.at[d, t - 1, i], rz.at[d, t - 1, i], to))
 
     def zwait(d, t, i):
         arrived(zref(d, t, i, t == NT), rz.at[d, t - 1, i])
 
     def dsend(d, t):
-        src = dn(z, t - 1, NZ) if d == 0 else up(z, t - 1, NZ)
-        go(rc(gd.at[src], gd.at[src], szd.at[d, t - 1], rzd.at[d, t - 1], dzr if d == 0 else dzl))
+        n = 2 if t == NT else t - 1
+        ref = gd.at[dn(z, n, NZ) if d == 0 else up(z, n, NZ)]
+        to = dz2r if t == NT else (dzr if d == 0 else dzl)
+        go(rc(ref, ref, szd.at[d, t - 1], rzd.at[d, t - 1], to))
 
     def dwait(d, t):
-        src = dn(z, t, NZ) if d == 0 else up(z, t, NZ)
-        arrived(gd.at[src], rzd.at[d, t - 1])
+        arrived(gd.at[dn(z, t, NZ) if d == 0 else up(z, t, NZ)], rzd.at[d, t - 1])
 
     def delta_rows(zc):
         tile = gd[zc]
@@ -267,39 +269,48 @@
     def dprob_late(h):
         dprob(h, NT, pl_[h], pair(do3, h, NT))
         kh = kv[:, h, 0].reshape(KV, HD)
-        dqa[h] = (nn(db[h], kh) * jnp.exp(m3[h] - lse3[h])).reshape(NZ, ZR, HD)
+        dqa[h] = nn(db[h], kh).reshape(NZ, ZR, HD)
 
     lane2 = lax.broadcasted_iota(jnp.int32, (RT, 128), 1)
 
-    mz = xh * NZ + z
+    def columns(rows_):
+        pad = jnp.zeros((128 - SR, 128), F32)
+        return jnp.concatenate([rows_, pad], axis=0).T
 
     def stats_send():
         st = jnp.zeros((RT, 128), F32)
         for h in range(HG):
             for rt in range(NR):
                 st = jnp.where(lane2 == h * NR + rt, lse3[h, rt * RT:(rt + 1) * RT], st)
-        lz[mz] = st.T[:SR]
-        for j in range(NZ):
-            for k in range(NX):
-                if (j, k) != (0, 0):
-                    to = dev(s, y, up(xh, k, NX), up(z, j, NZ))
-                    go(rc(lz.at[mz], lz.at[mz], sl.at[k, j], rl.at[k, j], to))
+        lx[0] = st.T[:SR]
+        go(rc(lx.at[0], lx.at[1], sx.at[0], rx.at[0], dev(s, y, up(xh, 1, NX), z)))
+
+    def stats_pair():
+        arrived(lx.at[1], rx.at[0])
+        a, b = lx[0], lx[1]
+        mx = jnp.maximum(a, b)
+        both = mx + jnp.log(jnp.exp(a - mx) + jnp.exp(b - mx))
+        lz[z] = both
+        for j in range(1, NZ):
+            go(rc(lz.at[z], lz.at[z], sl.at[j], rl.at[j], dev(s, y, xh, up(z, j, NZ))))
+        tt = columns(both)
+        for h in range(HG):
+            for rt in range(NR):
+                i = h * NR + rt
+                lse3[h, rt * RT:(rt + 1) * RT] = jnp.broadcast_to(tt[:, i:i + 1], (RT, 128))
 
     def stats_wait():
-        for j in range(NZ):
-            for k in range(NX):
-                if (j, k) != (0, 0):
-                    f = (up(xh, k, NX) << 3) | dn(z, j, NZ)
-                    arrived(lz.at[f], rl.at[k, j])
+        for j in range(1, NZ):
+            f = dn(z, j, NZ)
+            arrived(lz.at[f], rl.at[j])
         mx = lz[0]
-        for f in range(1, NX * NZ):
+        for f in range(1, NZ):
             mx = jnp.maximum(mx, lz[f])
         tot = jnp.exp(lz[0] - mx)
-        for f in range(1, NX * NZ):
+        for f in range(1, NZ):
             tot = tot + jnp.exp(lz[f] - mx)
         lt = mx + jnp.log(tot)
-        pad = jnp.zeros((128 - SR, 128), F32)
-        tt = jnp.concatenate([lt, pad], axis=0).T
+        tt = columns(lt)
         for h in range(HG):
             for rt in range(NR):
                 rows = slice(rt * RT, (rt + 1) * RT)
@@ -307,12 +318,11 @@
                 col = jnp.broadcast_to(tt[:, i:i + 1], (RT, 128))
                 c3[h, rows] = jnp.exp(m3[h, rows] - col)
                 w3[h, rows] = jnp.exp(lse3[h, rows] - col)
-        return lt, pad
-
-    def weights(lt, pad):
+        return lt
+
+    def weights(lt):
         for i, n in enumerate((-2, -1, 1, 2)):
-            f = (xh << 3) | up(z, n, NZ)
-            wt[i] = jnp.concatenate([jnp.exp(lz[f] - lt), pad], axis=0).T
+            wt[i] = columns(jnp.exp(lz[up(z, n, NZ)] - lt))
 
     lane3 = lax.broadcasted_iota(jnp.int32, (ZR, 128), 1)
 
@@ -344,16 +354,19 @@
         for i, (h0, n) in enumerate(PIECES):
             zwait(0, t - 1, i)
             zwait(1, t - 1, i)
-            if t <= NT:
-                zsend(0, t, i)
-                zsend(1, t, i)
+            for n_ in (t, t + 1):
+                if n_ == t < NT or n_ == NT == t + 1:
+                    zsend(0, n_, i)
+                    zsend(1, n_, i)
             if i == 0:
                 dwait(0, t - 1)
                 if t <= NT:
                     dwait(1, t - 1)
+                if t < NT:
                     dsend(0, t)
-                    if t < NT:
-                        dsend(1, t)
+                    dsend(1, t)
+                if t == NT - 1:
+                    dsend(0, NT)
                 for zc in chunks(t - 1):
                     delta_rows(zc)
             if t == 2:
@@ -365,7 +378,6 @@
     stats_send()
 
     HR = ZR // 2
-    dz2r, dz2l = dev(s, y, xh, up(z, 2, NZ)), dev(s, y, xh, dn(z, 2, NZ))
 
     def zmsg(d, kind):
         a_, b_ = zs.at[d, kind], zr_.at[d, kind]
@@ -379,6 +391,8 @@
         return up(z, n, NZ) if d == 0 else dn(z, n, NZ)
 
     def query_grads():
+        for h in range(HG):
+            dqa[h] = dqa[h] * jnp.exp(m3[h] - lse3[h]).reshape(NZ, ZR, HD)
         for kind, n in ((1, 3), (0, 4), (2, 1)):
             for d in range(2):
                 for h in range(HG):
@@ -426,39 +440,48 @@
         ks1[h, 0, 1] = dkv[h, yr, 1].astype(BF16)
         ks1[h, 1, 0] = dkv[h, y2, 1].astype(BF16)
         ks1[h, 1, 1] = dkv[h, yl, 0].astype(BF16)
-        go(rc(ks1.at[h, 0], kr1.at[h, 0], sk.at[0, 0, h], rk.at[0, 0, h], dyr))
-        go(rc(ks1.at[h, 1], kr1.at[h, 1], sk.at[0, 1, h], rk.at[0, 1, h], dyl))
+        go(leg(h, 0, 0, dyr))
+        go(leg(h, 1, 0, dyl))
+
+    def leg(h, d, i, to):
+        return rc(ks1.at[h, d, i], kr1.at[h, d, i], sk.at[i, d, h], rk.at[i, d, h], to)
+
+    def near_blocks(h):
+        go(leg(h, 0, 1, dyr))
+        go(leg(h, 1, 1, dyl))
 
     def second_leg(h):
-        arrived(kr1.at[h, 0], rk.at[0, 0, h])
+        arrived(kr1.at[h, 0, 0], rk.at[0, 0, h])
         ks2[h, 0] = (dkv[h, yr, 0] + kr1[h, 0, 0].astype(F32)).astype(BF16)
-        go(rc(ks2.at[h, 0], kr2.at[h, 0], sk.at[1, 0, h], rk.at[1, 0, h], dyr))
-        arrived(kr1.at[h, 1], rk.at[0, 1, h])
+        go(rc(ks2.at[h, 0], kr2.at[h, 0], sk.at[2, 0, h], rk.at[2, 0, h], dyr))
+        arrived(kr1.at[h, 1, 0], rk.at[0, 1, h])
         ks2[h, 1] = (dkv[h, yl, 1] + kr1[h, 1, 0].astype(F32)).astype(BF16)
-        go(rc(ks2.at[h, 1], kr2.at[h, 1], sk.at[1, 1, h], rk.at[1, 1, h], dyl))
+        go(rc(ks2.at[h, 1], kr2.at[h, 1], sk.at[2, 1, h], rk.at[2, 1, h], dyl))
 
     def cache_out(h):
-        arrived(kr2.at[h, 0], rk.at[1, 0, h])
-        arrived(kr2.at[h, 1], rk.at[1, 1, h])
+        arrived(kr1.at[h, 0, 1], rk.at[1, 0, h])
+        arrived(kr1.at[h, 1, 1], rk.at[1, 1, h])
+        arrived(kr2.at[h, 0], rk.at[2, 0, h])
+        arrived(kr2.at[h, 1], rk.at[2, 1, h])
         cols = slice(h * HD, (h + 1) * HD)
         dk_out[:, cols] = (dkv[h, y, 0] + kr1[h, 1, 1].astype(F32) + kr2[h, 0].astype(F32)).astype(BF16)
         dv_out[:, cols] = (dkv[h, y, 1] + kr1[h, 0, 1].astype(F32) + kr2[h, 1].astype(F32)).astype(BF16)
 
     for h in range(HG):
         dprob_late(h)
+    stats_pair()
     query_grads()
-    stats = stats_wait()
-    cache_grads(0)
-    cache_grads(1)
-    weights(*stats)
+    total = stats_wait()
+    for h in range(HG):
+        cache_grads(h)
+        if h > 0:
+            near_blocks(h - 1)
+    near_blocks(HG - 1)
+    weights(total)
     query_relay()
     second_leg(0)
-    cache_grads(2)
     second_leg(1)
-    cache_grads(3)
     second_leg(2)
-    cache_grads(4)
-    second_leg(3)
     query_sum()
 
     for j in range(NY):
@@ -478,7 +501,8 @@
     def _():
         p8[0, s] = tb[mine]
 
-    second_leg(HG - 1)
+    second_leg(3)
+    second_leg(4)
     for h in range(HG):
         cache_out(h)
 
@@ -521,7 +545,7 @@
         vm((NY, HG, 2, KR, HD), BF16), vm((HG, QW, HD), BF16), vm((HG, QW, HD), BF16), vm((QW, 128), F32),
         vm((HG, RT, KV), F32), vm((HG, QW, KV), BF16), vm((HG, QW, KV), BF16),
         vm((HG, QW, 128), F32), vm((HG, QW, 128), F32), vm((HG, QW, 128), F32),
-        vm((HG, QW, 128), F32), vm((NX * NZ, SR, 128), F32), vm((4, 128, 128), F32),
+        vm((HG, QW, 128), F32), vm((2, SR, 128), F32), vm((NZ, SR, 128), F32), vm((4, 128, 128), F32),
         vm((HG, NZ, ZR, HD), F32), vm((2, 4, HG, ZR, HD), BF16), vm((2, 4, HG, ZR, HD), BF16),
         vm((HG, NY, 2, KR, HD), F32),
         vm((HG, 2, 2, KR, HD), BF16), vm((HG, 2, 2, KR, HD), BF16),
@@ -530,8 +554,8 @@
         dma((5,)), dma((NS, NX)), dma((NX, NY)),
         dma((2, NT, 2)), dma((2, NT, 2)), dma((2, NT)), dma((2, NT)),
         dma((2, 2)), dma((2, 2)), dma((2, 2)), dma((2, 2)),
-        dma((NX, NZ)), dma((NX, NZ)), dma((2, 4)), dma((2, 4)),
-        dma((2, 2, HG)), dma((2, 2, HG)), dma((NY, NX)), dma((NX, NS)),
+        dma((NZ,)), dma((NZ,)), dma((1,)), dma((1,)), dma((2, 4)), dma((2, 4)),
+        dma((3, 2, HG)), dma((3, 2, HG)), dma((NY, NX)), dma((NX, NS)),
     ]
     vspec = pl.BlockSpec(memory_space=pltpu.VMEM)
     hbm = pl.BlockSpec(memory_space=pl.ANY)

time: 70.8 us -> 65.2 us (0.921); the launches traced: 69.6 us -> 65.1 us
  Pallas kernels: 68.9 us -> 64.5 us
    pallas_call x1, Pallas kernels: 67.2 us -> 62.7 us  [local(): pl.pallas_call(kernel, out_shape=(jax.ShapeDtypeStruct((1, QR, NS * GF),...]
where the time goes in v5:
time: 65.2 us; the launch traced here: 65.1 us
  Pallas kernels  64.5 us (99%)
    pallas_call x1, Pallas kernels, local(): pl.pallas_call(kernel, out_shape=(jax.ShapeDtypeStruct((1, QR, NS * GF),...  62.7 us
    pallas_call x1, Pallas kernels, local(): pl.pallas_call(place, out_shape=tuple((jax.ShapeDtypeStruct(v.shape, v.dt...  1.76 us

profile of v5, /device:TPU:1, one launch (start us, length us, event | category | flops | bytes accessed | tf_op | source)
XLA Modules:
  0.0 65.1 jit_solution(16348468187982910266)
XLA Ops:
  0.6 62.7 %shard_map.85 = (bf16[1,8,2560]{2,1,0:T(8,128)(2,1)}, bf16[128,640]{1,0:T(8,128)(2,1)}, bf16[128,640]{1,0:T(8,128)(2,1)}) custom-call(s32[64]{0:T(128)} %order.1, bf16[1,8,2560]{2,1,0:T(8,128)(2,1)} %q_in.1, bf16[1,8,2560]{2,1,0:T(8,128)(2,1)} %do_in.1, bf16[1,8,2560]{2,1,0:T(8,128)(2,1)} %o_in.1, bf16[128,640]{1,0:T(8,128)(2,1)} %k_in.1, bf16[128,640]{1,0:T(8,128)(2,1)} %v_in.1), custom_call_target="tpu_custom_call" | custom-call | tf_op jit(solution)/shard_map/pallas_call | solution.py:562
  63.3 1.8 %shard_map.86 = (bf16[1,8,2560]{2,1,0:T(8,128)(2,1)}, bf16[128,640]{1,0:T(8,128)(2,1)}, bf16[128,640]{1,0:T(8,128)(2,1)}) custom-call(bf16[1,8,2560]{2,1,0:T(8,128)(2,1)} %get-tuple-element.6.a, bf16[128,640]{1,0:T(8,128)(2,1)} %get-tuple-element.7.b, bf16[128,640]{1,0:T(8,128)(2,1)} %get-tuple-element.8.c), custom_call_target="tpu_custom_call" | custom-call | tf_op jit(solution)/shard_map/pallas_call | solution.py:575

commit v6 on v5

--- a/solution.py
+++ b/solution.py
@@ -23,7 +23,7 @@
 RT = 128
 NR = QW // RT
 PIECES = ((0, 2), (2, 3))
-SR = 24
+SROWS = (8, 16)
 
 
 def nt(a, b):
@@ -39,7 +39,7 @@
 
 
 def kernel(order, q_in, do_in, o_in, k_in, v_in, dq_out, dk_out, dv_out,
-           qv, dov, ov, kin, vin, pk, p1, g, gd, kv, q3, do3, delc, pl_, pb, db, m3, lse3, c3, w3, lx, lz, wt,
+           qv, dov, ov, kin, vin, pk, p1, g, gd, kv, q3, do3, delc, pl_, pb, db, m3, lse3, c3, lx, lz, wt,
            dqa, zs, zr_, dkv, ks1, kr1, ks2, kr2, tb, p8,
            sin, s1, r1, sz, rz, szd, rzd, sy, ry, sf, rf, sl, rl, sx, rx, sg, rg, sk, rk, s8, r8):
     s = lax.axis_index("section")
@@ -72,6 +72,11 @@
     def go(cp):
         cp.start()
         sends.append(cp)
+
+    def settle(count_):
+        for cp in sends[:count_]:
+            cp.wait_send()
+        del sends[:count_]
 
     loads = []
     for i, (a, b) in enumerate(((q_in, qv), (do_in, dov), (o_in, ov), (k_in, kin), (v_in, vin))):
@@ -274,62 +279,68 @@
     lane2 = lax.broadcasted_iota(jnp.int32, (RT, 128), 1)
 
     def columns(rows_):
-        pad = jnp.zeros((128 - SR, 128), F32)
+        pad = jnp.zeros((128 - rows_.shape[0], 128), F32)
         return jnp.concatenate([rows_, pad], axis=0).T
 
-    def stats_send():
+    def heads_of(i):
+        return range(PIECES[i][0], PIECES[i][0] + PIECES[i][1])
+
+    def stats_send(i):
         st = jnp.zeros((RT, 128), F32)
-        for h in range(HG):
+        for j, h in enumerate(heads_of(i)):
             for rt in range(NR):
-                st = jnp.where(lane2 == h * NR + rt, lse3[h, rt * RT:(rt + 1) * RT], st)
-        lx[0] = st.T[:SR]
-        go(rc(lx.at[0], lx.at[1], sx.at[0], rx.at[0], dev(s, y, up(xh, 1, NX), z)))
-
-    def stats_pair():
-        arrived(lx.at[1], rx.at[0])
-        a, b = lx[0], lx[1]
+                st = jnp.where(lane2 == j * NR + rt, lse3[h, rt * RT:(rt + 1) * RT], st)
+        sr = pl.ds(0, SROWS[i])
+        lx[i, 0, sr] = st.T[:SROWS[i]]
+        go(rc(lx.at[i, 0, sr], lx.at[i, 1, sr], sx.at[i], rx.at[i], dev(s, y, up(xh, 1, NX), z)))
+
+    def stats_pair(i):
+        sr = pl.ds(0, SROWS[i])
+        arrived(lx.at[i, 1, sr], rx.at[i])
+        a, b = lx[i, 0, sr], lx[i, 1, sr]
         mx = jnp.maximum(a, b)
         both = mx + jnp.log(jnp.exp(a - mx) + jnp.exp(b - mx))
-        lz[z] = both
+        lz[i, z, sr] = both
         for j in range(1, NZ):
-            go(rc(lz.at[z], lz.at[z], sl.at[j], rl.at[j], dev(s, y, xh, up(z, j, NZ))))
+            ref = lz.at[i, z, sr]
+            go(rc(ref, ref, sl.at[i, j], rl.at[i, j], dev(s, y, xh, up(z, j, NZ))))
         tt = columns(both)
-        for h in range(HG):
+        for j, h in enumerate(heads_of(i)):
             for rt in range(NR):
-                i = h * NR + rt
-                lse3[h, rt * RT:(rt + 1) * RT] = jnp.broadcast_to(tt[:, i:i + 1], (RT, 128))
-
-    def stats_wait():
+                k = j * NR + rt
+                lse3[h, rt * RT:(rt + 1) * RT] = jnp.broadcast_to(tt[:, k:k + 1], (RT, 128))
+
+    def stats_wait(i):
+        sr = pl.ds(0, SROWS[i])
         for j in range(1, NZ):
-            f = dn(z, j, NZ)
-            arrived(lz.at[f], rl.at[j])
-        mx = lz[0]
+            arrived(lz.at[i, dn(z, j, NZ), sr], rl.at[i, j])
+        mx = lz[i, 0, sr]
         for f in range(1, NZ):
-            mx = jnp.maximum(mx, lz[f])
-        tot = jnp.exp(lz[0] - mx)
+            mx = jnp.maximum(mx, lz[i, f, sr])
+        tot = jnp.exp(lz[i, 0, sr] - mx)
         for f in range(1, NZ):
-            tot = tot + jnp.exp(lz[f] - mx)
+            tot = tot + jnp.exp(lz[i, f, sr] - mx)
         lt = mx + jnp.log(tot)
         tt = columns(lt)
-        for h in range(HG):
+        for j, h in enumerate(heads_of(i)):
             for rt in range(NR):
                 rows = slice(rt * RT, (rt + 1) * RT)
-                i = h * NR + rt
-                col = jnp.broadcast_to(tt[:, i:i + 1], (RT, 128))
+                k = j * NR + rt
+                col = jnp.broadcast_to(tt[:, k:k + 1], (RT, 128))
                 c3[h, rows] = jnp.exp(m3[h, rows] - col)
-                w3[h, rows] = jnp.exp(lse3[h, rows] - col)
         return lt
 
-    def weights(lt):
-        for i, n in enumerate((-2, -1, 1, 2)):
-            wt[i] = columns(jnp.exp(lz[up(z, n, NZ)] - lt))
+    def weights(i, lt):
+        sr = pl.ds(0, SROWS[i])
+        for k, n in enumerate((-2, -1, 0, 1, 2)):
+            wt[i, k] = columns(jnp.exp(lz[i, up(z, n, NZ), sr] - lt))
 
     lane3 = lax.broadcasted_iota(jnp.int32, (ZR, 128), 1)
 
     def weight(n, zc, h):
-        i = {-2: 0, -1: 1, 1: 2, 2: 3}[n]
-        v = wt[i, pl.ds(pl.multiple_of((zc & 1) * ZR, ZR), ZR)]
-        v = jnp.where(lane3 == h * NR + (zc >> 1), v, 0.0)
+        i = 0 if h < PIECES[1][0] else 1
+        v = wt[i, n + 2, pl.ds(pl.multiple_of((zc & 1) * ZR, ZR), ZR)]
+        v = jnp.where(lane3 == (h - PIECES[i][0]) * NR + (zc >> 1), v, 0.0)
         return jnp.sum(v, axis=1, keepdims=True)
 
     for h in range(HG):
@@ -375,55 +386,60 @@
                 kv_ready(i)
             for h in range(h0, h0 + n):
                 score_tile(h, t - 1)
-    stats_send()
+            if t == NT + 1:
+                if i == 0:
+                    ring_sends = len(sends)
+                stats_send(i)
 
     HR = ZR // 2
 
-    def zmsg(d, kind):
-        a_, b_ = zs.at[d, kind], zr_.at[d, kind]
+    def zmsg(d, kind, i):
+        hs = pl.ds(*PIECES[i])
+        a_, b_ = zs.at[d, kind, hs], zr_.at[d, kind, hs]
         if kind == 0:
             part = pl.ds(d * HR, HR)
-            a_, b_ = zs.at[d, kind, :, part], zr_.at[d, kind, :, part]
+            a_, b_ = zs.at[d, kind, hs, part], zr_.at[d, kind, hs, part]
         near, far = (dzr, dz2r) if d == 0 else (dzl, dz2l)
-        return rc(a_, b_, sg.at[d, kind], rg.at[d, kind], far if kind in (0, 3) else near)
+        return rc(a_, b_, sg.at[d, kind, i], rg.at[d, kind, i], far if kind in (0, 3) else near)
 
     def step(d, n):
         return up(z, n, NZ) if d == 0 else dn(z, n, NZ)
 
-    def query_grads():
-        for h in range(HG):
+    def query_scale(i):
+        for h in heads_of(i):
             dqa[h] = dqa[h] * jnp.exp(m3[h] - lse3[h]).reshape(NZ, ZR, HD)
-        for kind, n in ((1, 3), (0, 4), (2, 1)):
-            for d in range(2):
-                for h in range(HG):
-                    if kind == 0:
-                        part = slice(d * HR, (d + 1) * HR)
-                        zs[d, kind, h, part] = dqa[h, step(d, n), part].astype(BF16)
-                    else:
-                        zs[d, kind, h] = dqa[h, step(d, n)].astype(BF16)
-                go(zmsg(d, kind))
-
-    def query_relay():
+
+    def query_send(i, kind, n):
+        for d in range(2):
+            for h in heads_of(i):
+                if kind == 0:
+                    part = slice(d * HR, (d + 1) * HR)
+                    zs[d, kind, h, part] = dqa[h, step(d, n), part].astype(BF16)
+                else:
+                    zs[d, kind, h] = dqa[h, step(d, n)].astype(BF16)
+            go(zmsg(d, kind, i))
+
+    def query_relay(i):
         for d in range(2):
             sign = 1 - 2 * d
-            zmsg(d, 0).wait_recv()
-            zmsg(d, 1).wait_recv()
+            zmsg(d, 0, i).wait_recv()
+            zmsg(d, 1, i).wait_recv()
             part = slice(d * HR, (d + 1) * HR)
             rest = slice((1 - d) * HR, (2 - d) * HR)
             to = step(d, 2)
-            for h in range(HG):
-                acc = dqa[h, to] * w3[h, rowsof(to)] + zr_[d, 1, h].astype(F32) * weight(-sign, to, h)
+            for h in heads_of(i):
+                acc = dqa[h, to] * weight(0, to, h) + zr_[d, 1, h].astype(F32) * weight(-sign, to, h)
                 far = zr_[d, 0, h, part].astype(F32) * weight(-2 * sign, to, h)[part]
                 zs[d, 3, h, rest] = acc[rest].astype(BF16)
                 zs[d, 3, h, part] = (acc[part] + far).astype(BF16)
-            go(zmsg(d, 3))
-
-    def query_sum():
+            go(zmsg(d, 3, i))
+
+    def query_sum(i):
         for d in range(2):
-            zmsg(d, 2).wait_recv()
-            zmsg(d, 3).wait_recv()
-        for h in range(HG):
-            acc = dqa[h, z] * w3[h, rowsof(z)]
+            zmsg(d, 2, i).wait_recv()
+            zmsg(d, 3, i).wait_recv()
+        for h in heads_of(i):
+            acc = dqa[h, z] * weight(0, z, h)
             for d in range(2):
                 acc = acc + zr_[d, 3, h].astype(F32)
                 acc = acc + zr_[d, 2, h].astype(F32) * weight(2 * d - 1, z, h)
@@ -467,22 +483,46 @@
         dk_out[:, cols] = (dkv[h, y, 0] + kr1[h, 1, 1].astype(F32) + kr2[h, 0].astype(F32)).astype(BF16)
         dv_out[:, cols] = (dkv[h, y, 1] + kr1[h, 0, 1].astype(F32) + kr2[h, 1].astype(F32)).astype(BF16)
 
-    for h in range(HG):
+    dprob_late(0)
+    settle(ring_sends)
+    stats_pair(0)
+    for h in heads_of(0):
+        if h > 0:
+            dprob_late(h)
+    query_scale(0)
+    query_send(0, 1, 3)
+    query_send(0, 0, 4)
+    stats_pair(1)
+    for h in heads_of(1):
         dprob_late(h)
-    stats_pair()
-    query_grads()
-    total = stats_wait()
-    for h in range(HG):
-        cache_grads(h)
-        if h > 0:
-            near_blocks(h - 1)
-    near_blocks(HG - 1)
-    weights(total)
-    query_relay()
+    query_scale(1)
+    query_send(1, 1, 3)
+    query_send(1, 0, 4)
+    early = len(sends)
+    query_send(0, 2, 1)
+    query_send(1, 2, 1)
+    total = stats_wait(0)
+    cache_grads(0)
+    weights(0, total)
+    query_relay(0)
+    near_blocks(0)
+    cache_grads(1)
+    near_blocks(1)
+    total = stats_wait(1)
+    cache_grads(2)
+    near_blocks(2)
+    weights(1, total)
+    query_relay(1)
+    cache_grads(3)
+    near_blocks(3)
+    cache_grads(4)
+    near_blocks(4)
+    settle(early)
     second_leg(0)
+    query_sum(0)
     second_leg(1)
     second_leg(2)
-    query_sum()
+    query_sum(1)
 
     for j in range(NY):
         for k in range(NX):
@@ -545,7 +585,7 @@
         vm((NY, HG, 2, KR, HD), BF16), vm((HG, QW, HD), BF16), vm((HG, QW, HD), BF16), vm((QW, 128), F32),
         vm((HG, RT, KV), F32), vm((HG, QW, KV), BF16), vm((HG, QW, KV), BF16),
         vm((HG, QW, 128), F32), vm((HG, QW, 128), F32), vm((HG, QW, 128), F32),
-        vm((HG, QW, 128), F32), vm((2, SR, 128), F32), vm((NZ, SR, 128), F32), vm((4, 128, 128), F32),
+        vm((2, 2, 16, 128), F32), vm((2, NZ, 16, 128), F32), vm((2, 5, 128, 128), F32),
         vm((HG, NZ, ZR, HD), F32), vm((2, 4, HG, ZR, HD), BF16), vm((2, 4, HG, ZR, HD), BF16),
         vm((HG, NY, 2, KR, HD), F32),
         vm((HG, 2, 2, KR, HD), BF16), vm((HG, 2, 2, KR, HD), BF16),
@@ -554,7 +594,7 @@
         dma((5,)), dma((NS, NX)), dma((NX, NY)),
         dma((2, NT, 2)), dma((2, NT, 2)), dma((2, NT)), dma((2, NT)),
         dma((2, 2)), dma((2, 2)), dma((2, 2)), dma((2, 2)),
-        dma((NZ,)), dma((NZ,)), dma((1,)), dma((1,)), dma((2, 4)), dma((2, 4)),
+        dma((2, NZ)), dma((2, NZ)), dma((2,)), dma((2,)), dma((2, 4, 2)), dma((2, 4, 2)),
         dma((3, 2, HG)), dma((3, 2, HG)), dma((NY, NX)), dma((NX, NS)),
     ]
     vspec = pl.BlockSpec(memory_space=pltpu.VMEM)

time: 65.2 us -> 63.8 us (0.979)
  Pallas kernels: 64.5 us -> 62.7 us
    pallas_call x1, Pallas kernels: 62.7 us -> 61 us  [local(): pl.pallas_call(kernel, out_shape=(jax.ShapeDtypeStruct((1, QR, NS * GF),...]
where the time goes in v6:
time: 63.8 us; the launch traced here: 63.4 us
  Pallas kernels  62.7 us (98%)
  between operations  0.64 us (1%)
    pallas_call x1, Pallas kernels, local(): pl.pallas_call(kernel, out_shape=(jax.ShapeDtypeStruct((1, QR, NS * GF),...  61 us
    pallas_call x1, Pallas kernels, local(): pl.pallas_call(place, out_shape=tuple((jax.ShapeDtypeStruct(v.shape, v.dt...  1.76 us

profile of v6, /device:TPU:1, one launch (start us, length us, event | category | flops | bytes accessed | tf_op | source)
XLA Modules:
  0.0 63.4 jit_solution(9392679264776126572)
XLA Ops:
  0.6 61.0 %shard_map.85 = (bf16[1,8,2560]{2,1,0:T(8,128)(2,1)}, bf16[128,640]{1,0:T(8,128)(2,1)}, bf16[128,640]{1,0:T(8,128)(2,1)}) custom-call(s32[64]{0:T(128)} %order.1, bf16[1,8,2560]{2,1,0:T(8,128)(2,1)} %q_in.1, bf16[1,8,2560]{2,1,0:T(8,128)(2,1)} %do_in.1, bf16[1,8,2560]{2,1,0:T(8,128)(2,1)} %o_in.1, bf16[128,640]{1,0:T(8,128)(2,1)} %k_in.1, bf16[128,640]{1,0:T(8,128)(2,1)} %v_in.1), custom_call_target="tpu_custom_call" | custom-call | tf_op jit(solution)/shard_map/pallas_call | solution.py:602
  61.6 1.8 %shard_map.86 = (bf16[1,8,2560]{2,1,0:T(8,128)(2,1)}, bf16[128,640]{1,0:T(8,128)(2,1)}, bf16[128,640]{1,0:T(8,128)(2,1)}) custom-call(bf16[1,8,2560]{2,1,0:T(8,128)(2,1)} %get-tuple-element.6.a, bf16[128,640]{1,0:T(8,128)(2,1)} %get-tuple-element.7.b, bf16[128,640]{1,0:T(8,128)(2,1)} %get-tuple-element.8.c), custom_call_target="tpu_custom_call" | custom-call | tf_op jit(solution)/shard_map/pallas_call | solution.py:615

commit v7 on v6

--- a/solution.py
+++ b/solution.py
@@ -361,14 +361,23 @@
             dsend(0, 1)
             dsend(1, 1)
     kv_forward(0)
+    def score_piece(t, i):
+        if t == 1:
+            kv_ready(i)
+        if i == 0:
+            for zc in chunks(t):
+                delta_rows(zc)
+        for h in heads_of(i):
+            score_tile(h, t)
+
+    pending = []
     for t in range(2, NT + 2):
-        for i, (h0, n) in enumerate(PIECES):
-            zwait(0, t - 1, i)
-            zwait(1, t - 1, i)
-            for n_ in (t, t + 1):
-                if n_ == t < NT or n_ == NT == t + 1:
-                    zsend(0, n_, i)
-                    zsend(1, n_, i)
+        for i in range(2):
+            for d in range(2):
+                zwait(d, t - 1, i)
+                for n_ in (t, t + 1):
+                    if n_ == t < NT or n_ == NT == t + 1:
+                        zsend(d, n_, i)
             if i == 0:
                 dwait(0, t - 1)
                 if t <= NT:
@@ -378,14 +387,11 @@
                     dsend(1, t)
                 if t == NT - 1:
                     dsend(0, NT)
-                for zc in chunks(t - 1):
-                    delta_rows(zc)
-            if t == 2:
-                if i == 0:
+                if t == 2:
                     kv_forward(1)
-                kv_ready(i)
-            for h in range(h0, h0 + n):
-                score_tile(h, t - 1)
+            pending.append((t - 1, i))
+            while len(pending) > (2 if (t, i) < (NT - 1, 1) else 0):
+                score_piece(*pending.pop(0))
             if t == NT + 1:
                 if i == 0:
                     ring_sends = len(sends)

time: 63.8 us -> 61.6 us (0.966)
  Pallas kernels: 62.7 us -> 60.9 us
    pallas_call x1, Pallas kernels: 61 us -> 59.1 us  [local(): pl.pallas_call(kernel, out_shape=(jax.ShapeDtypeStruct((1, QR, NS * GF),...]
where the time goes in v7:
time: 61.6 us; the launch traced here: 61.5 us
  Pallas kernels  60.9 us (99%)
  between operations  0.64 us (1%)
    pallas_call x1, Pallas kernels, local(): pl.pallas_call(kernel, out_shape=(jax.ShapeDtypeStruct((1, QR, NS * GF),...  59.1 us
    pallas_call x1, Pallas kernels, local(): pl.pallas_call(place, out_shape=tuple((jax.ShapeDtypeStruct(v.shape, v.dt...  1.76 us

profile of v7, /device:TPU:1, one launch (start us, length us, event | category | flops | bytes accessed | tf_op | source)
XLA Modules:
  0.0 61.5 jit_solution(3350038760195724661)
XLA Ops:
  0.6 59.1 %shard_map.85 = (bf16[1,8,2560]{2,1,0:T(8,128)(2,1)}, bf16[128,640]{1,0:T(8,128)(2,1)}, bf16[128,640]{1,0:T(8,128)(2,1)}) custom-call(s32[64]{0:T(128)} %order.1, bf16[1,8,2560]{2,1,0:T(8,128)(2,1)} %q_in.1, bf16[1,8,2560]{2,1,0:T(8,128)(2,1)} %do_in.1, bf16[1,8,2560]{2,1,0:T(8,128)(2,1)} %o_in.1, bf16[128,640]{1,0:T(8,128)(2,1)} %k_in.1, bf16[128,640]{1,0:T(8,128)(2,1)} %v_in.1), custom_call_target="tpu_custom_call" | custom-call | tf_op jit(solution)/shard_map/pallas_call | solution.py:608
  59.7 1.8 %shard_map.86 = (bf16[1,8,2560]{2,1,0:T(8,128)(2,1)}, bf16[128,640]{1,0:T(8,128)(2,1)}, bf16[128,640]{1,0:T(8,128)(2,1)}) custom-call(bf16[1,8,2560]{2,1,0:T(8,128)(2,1)} %get-tuple-element.6.a, bf16[128,640]{1,0:T(8,128)(2,1)} %get-tuple-element.7.b, bf16[128,640]{1,0:T(8,128)(2,1)} %get-tuple-element.8.c), custom_call_target="tpu_custom_call" | custom-call | tf_op jit(solution)/shard_map/pallas_call | solution.py:621

commit v8 on v7

--- a/solution.py
+++ b/solution.py
@@ -150,14 +150,17 @@
         p1[mine] = pk[s]
 
     dyr, dyl = dev(s, yr, xh, z), dev(s, yl, xh, z)
+
+    def kv_send(i):
+        ref = kv.at[y, pl.ds(*PIECES[i])]
+        go(rc(ref, ref, sy.at[0, i], ry.at[0, i], dyr))
+        go(rc(ref, ref, sy.at[1, i], ry.at[1, i], dyl))
+
     for h in range(HG):
         kv[y, h, 0] = kin[:, h * HD:(h + 1) * HD]
         kv[y, h, 1] = vin[:, h * HD:(h + 1) * HD]
-        for i, (h0, n) in enumerate(PIECES):
-            if h == h0 + n - 1:
-                ref = kv.at[y, pl.ds(h0, n)]
-                go(rc(ref, ref, sy.at[0, i], ry.at[0, i], dyr))
-                go(rc(ref, ref, sy.at[1, i], ry.at[1, i], dyl))
+        if h == PIECES[0][1] - 1:
+            kv_send(0)
 
     def kv_forward(i):
         hs = pl.ds(*PIECES[i])
@@ -360,6 +363,7 @@
         if i == 0:
             dsend(0, 1)
             dsend(1, 1)
+    kv_send(1)
     kv_forward(0)
     def score_piece(t, i):
         if t == 1:
@@ -516,12 +520,12 @@
     near_blocks(1)
     total = stats_wait(1)
     cache_grads(2)
-    near_blocks(2)
     weights(1, total)
     query_relay(1)
+    near_blocks(2)
     cache_grads(3)
+    cache_grads(4)
     near_blocks(3)
-    cache_grads(4)
     near_blocks(4)
     settle(early)
     second_leg(0)

time: 61.6 us -> 61.4 us (level)
  no operation moved by 1% of the time
where the time goes in v8:
time: 61.4 us; the launch traced here: 61.1 us
  Pallas kernels  60.5 us (99%)
  between operations  0.64 us (1%)
    pallas_call x1, Pallas kernels, local(): pl.pallas_call(kernel, out_shape=(jax.ShapeDtypeStruct((1, QR, NS * GF),...  58.7 us
    pallas_call x1, Pallas kernels, local(): pl.pallas_call(place, out_shape=tuple((jax.ShapeDtypeStruct(v.shape, v.dt...  1.76 us

profile of v8, /device:TPU:1, one launch (start us, length us, event | category | flops | bytes accessed | tf_op | source)
XLA Modules:
  0.0 61.1 jit_solution(12206660041267867774)
XLA Ops:
  0.6 58.7 %shard_map.85 = (bf16[1,8,2560]{2,1,0:T(8,128)(2,1)}, bf16[128,640]{1,0:T(8,128)(2,1)}, bf16[128,640]{1,0:T(8,128)(2,1)}) custom-call(s32[64]{0:T(128)} %order.1, bf16[1,8,2560]{2,1,0:T(8,128)(2,1)} %q_in.1, bf16[1,8,2560]{2,1,0:T(8,128)(2,1)} %do_in.1, bf16[1,8,2560]{2,1,0:T(8,128)(2,1)} %o_in.1, bf16[128,640]{1,0:T(8,128)(2,1)} %k_in.1, bf16[128,640]{1,0:T(8,128)(2,1)} %v_in.1), custom_call_target="tpu_custom_call" | custom-call | tf_op jit(solution)/shard_map/pallas_call | solution.py:612
  59.4 1.8 %shard_map.86 = (bf16[1,8,2560]{2,1,0:T(8,128)(2,1)}, bf16[128,640]{1,0:T(8,128)(2,1)}, bf16[128,640]{1,0:T(8,128)(2,1)}) custom-call(bf16[1,8,2560]{2,1,0:T(8,128)(2,1)} %get-tuple-element.6.a, bf16[128,640]{1,0:T(8,128)(2,1)} %get-tuple-element.7.b, bf16[128,640]{1,0:T(8,128)(2,1)} %get-tuple-element.8.c), custom_call_target="tpu_custom_call" | custom-call | tf_op jit(solution)/shard_map/pallas_call | solution.py:625

commit v9 on v8

--- a/solution.py
+++ b/solution.py
@@ -525,12 +525,12 @@
     near_blocks(2)
     cache_grads(3)
     cache_grads(4)
+    second_leg(0)
     near_blocks(3)
+    second_leg(1)
     near_blocks(4)
+    query_sum(0)
     settle(early)
-    second_leg(0)
-    query_sum(0)
-    second_leg(1)
     second_leg(2)
     query_sum(1)
 

time: 61.4 us -> 61.3 us (level)
  no operation moved by 1% of the time
where the time goes in v9:
time: 61.3 us; the launch traced here: 61.1 us
  Pallas kernels  60.5 us (99%)
  between operations  0.64 us (1%)
    pallas_call x1, Pallas kernels, local(): pl.pallas_call(kernel, out_shape=(jax.ShapeDtypeStruct((1, QR, NS * GF),...  58.7 us
    pallas_call x1, Pallas kernels, local(): pl.pallas_call(place, out_shape=tuple((jax.ShapeDtypeStruct(v.shape, v.dt...  1.76 us

profile of v9, /device:TPU:1, one launch (start us, length us, event | category | flops | bytes accessed | tf_op | source)
XLA Modules:
  0.0 61.1 jit_solution(7725405415990097361)
XLA Ops:
  0.6 58.7 %shard_map.85 = (bf16[1,8,2560]{2,1,0:T(8,128)(2,1)}, bf16[128,640]{1,0:T(8,128)(2,1)}, bf16[128,640]{1,0:T(8,128)(2,1)}) custom-call(s32[64]{0:T(128)} %order.1, bf16[1,8,2560]{2,1,0:T(8,128)(2,1)} %q_in.1, bf16[1,8,2560]{2,1,0:T(8,128)(2,1)} %do_in.1, bf16[1,8,2560]{2,1,0:T(8,128)(2,1)} %o_in.1, bf16[128,640]{1,0:T(8,128)(2,1)} %k_in.1, bf16[128,640]{1,0:T(8,128)(2,1)} %v_in.1), custom_call_target="tpu_custom_call" | custom-call | tf_op jit(solution)/shard_map/pallas_call | solution.py:612
  59.4 1.8 %shard_map.86 = (bf16[1,8,2560]{2,1,0:T(8,128)(2,1)}, bf16[128,640]{1,0:T(8,128)(2,1)}, bf16[128,640]{1,0:T(8,128)(2,1)}) custom-call(bf16[1,8,2560]{2,1,0:T(8,128)(2,1)} %get-tuple-element.6.a, bf16[128,640]{1,0:T(8,128)(2,1)} %get-tuple-element.7.b, bf16[128,640]{1,0:T(8,128)(2,1)} %get-tuple-element.8.c), custom_call_target="tpu_custom_call" | custom-call | tf_op jit(solution)/shard_map/pallas_call | solution.py:625
